TPU v7x, 512 devices: a whole 4x8x8 slice. The times are simulated.
512 devices in a mesh: seq: 128 (over y, z_hi, x), head: 4 (over z_lo, core).
Axes of the slice: x: 4, y: 8, z: 8 (z_hi: 4, z_lo: 2; z = z_hi * 2 + z_lo), core: 2. Of those that a mesh axis runs over, the one named last changes fastest.
Arguments:
- fixed_point: bfloat16 [16384, 2048], P('seq'), may hold values from -7 to 7
- upstream: bfloat16 [16384, 2048], P('seq'), may hold values from -70 to 70
- norm_gain: float32 [2048], replicated, may hold values from 0.7 to 1.3
- query_weight: bfloat16 [2048, 1024], P(None, 'head'), may hold values from -0.35355339 to 0.35355339
- keyval_weight: bfloat16 [2048, 512], P(None, 'head'), may hold values from -0.143631065 to 0.143631065
- output_weight: bfloat16 [1024, 2048], P('head'), may hold values from -0.09375 to 0.09375
- log_norm: float32 [16, 16384], P('head', 'seq'), as said below
- attention_out: bfloat16 [16384, 1024], P('seq', 'head'), as said below
Outputs:
- adjoint: float32 [16384, 2048], P('seq')
Inputs may be any that keep to these rules, and one draw needn't show every extreme that they name: attention_out[t, h] is the sum over the keys that query t sees of exp(scores[h, t, j] - log_norm[h, t]) v_c(j), rounded to bfloat16.
All inputs are finite; a program needn't handle non-finite values.
Results may differ from a plain program's by a relative error of at most 0.012.
The roundings to bfloat16 on the way count: a program that leaves them out, or rounds other values in their place, can miss the bound.
Values may be sent and summed in bfloat16 or wider, within the bound.
A program may use at most 64 MiB of HBM per device.

v0:
```python
import jax
import jax.numpy as jnp
from jax import lax
from jax.sharding import PartitionSpec as P

WIN_DEVS = 4
ITERS = 3


norm_eps = 1e-05
mix_eps = 1e-06


def shifted(value, axis, steps):
    count = lax.axis_size(axis)
    initial, last = (max(0, -steps), min(count, count - steps))
    return lax.ppermute(value, axis, [(source, source + steps) for source in range(initial, last)])


def shards(
    fixed_point,
    upstream,
    norm_gain,
    query_weight,
    keyval_weight,
    output_weight,
    log_norm,
    attention_out,
):
    row_count, model_width = fixed_point.shape
    head_width = keyval_weight.shape[1] // 2
    local_heads = log_norm.shape[0]
    score_scale = head_width ** (-0.5)
    latent = fixed_point.astype(jnp.float32)
    inverse = lax.rsqrt(jnp.mean(latent * latent, axis=1, keepdims=True) + norm_eps)
    normed = latent * inverse
    hidden = (normed * norm_gain).astype(jnp.bfloat16)
    queries = jnp.dot(hidden, query_weight, preferred_element_type=jnp.float32).astype(jnp.bfloat16)
    keyval = jnp.dot(hidden, keyval_weight, preferred_element_type=jnp.float32).astype(jnp.bfloat16)
    token_block = lax.axis_index("seq")
    earlier = []
    for offset in range(WIN_DEVS, 0, -1):
        earlier.append(shifted(keyval, "seq", offset))
    window_keys = jnp.concatenate(earlier + [keyval], axis=0)
    key_rows = window_keys[:, :head_width]
    value_rows = window_keys[:, head_width:]
    query_heads = queries.reshape(row_count, local_heads, head_width)
    key_pos = jnp.arange((WIN_DEVS + 1) * row_count)[None, :]
    query_pos = jnp.arange(row_count)[:, None]
    allowed = (key_pos > query_pos) & (key_pos <= query_pos + WIN_DEVS * row_count)
    allowed = allowed & (key_pos >= (WIN_DEVS - token_block) * row_count)
    saved_out = attention_out.astype(jnp.float32).reshape(row_count, local_heads, head_width)
    cotangent = upstream.astype(jnp.float32)
    entries = row_count * lax.axis_size("seq") * model_width
    last_image = cotangent
    last_residual = cotangent
    current = cotangent
    for offset in range(ITERS):
        adjoint_grad_out = jnp.dot(
            current.astype(jnp.bfloat16), output_weight.T, preferred_element_type=jnp.float32
        )
        scores = (
            jnp.einsum("rhe,pe->hrp", query_heads, key_rows, preferred_element_type=jnp.float32)
            * score_scale
        )
        weights_now = jnp.where(allowed[None], jnp.exp(scores - log_norm[:, :, None]), 0.0).astype(
            jnp.bfloat16
        )
        grad_outb = adjoint_grad_out.astype(jnp.bfloat16).reshape(
            row_count, local_heads, head_width
        )
        row_terms = jnp.sum(
            adjoint_grad_out.reshape(row_count, local_heads, head_width) * saved_out, axis=2
        ).T
        grad_prob = jnp.einsum(
            "rhe,pe->hrp", grad_outb, value_rows, preferred_element_type=jnp.float32
        )
        grad_score = (weights_now.astype(jnp.float32) * (grad_prob - row_terms[:, :, None])).astype(
            jnp.bfloat16
        )
        grad_query = (
            jnp.einsum("hrp,pe->rhe", grad_score, key_rows, preferred_element_type=jnp.float32)
            * score_scale
        )
        grad_query = grad_query.astype(jnp.bfloat16).reshape(row_count, local_heads * head_width)
        grad_key = (
            jnp.einsum("hrp,rhe->pe", grad_score, query_heads, preferred_element_type=jnp.float32)
            * score_scale
        )
        grad_value = jnp.einsum(
            "hrp,rhe->pe", weights_now, grad_outb, preferred_element_type=jnp.float32
        )
        key_terms = jnp.concatenate([grad_key, grad_value], axis=1)
        collected = key_terms[WIN_DEVS * row_count :]
        for attention_offset in range(1, WIN_DEVS + 1):
            first_row = (WIN_DEVS - attention_offset) * row_count
            arrived = shifted(
                key_terms[first_row : first_row + row_count].astype(jnp.bfloat16),
                "seq",
                -attention_offset,
            ).astype(jnp.float32)
            collected = collected + arrived
        grad_keyval = collected.astype(jnp.bfloat16)
        partial_value = jnp.dot(grad_query, query_weight.T, preferred_element_type=jnp.float32)
        running = lax.psum(
            (
                partial_value
                + jnp.dot(grad_keyval, keyval_weight.T, preferred_element_type=jnp.float32)
            ).astype(jnp.bfloat16),
            "head",
        ).astype(jnp.float32)
        scaled = running * norm_gain
        mapped = cotangent + inverse * (
            scaled - normed * jnp.mean(scaled * normed, axis=1, keepdims=True)
        )
        residual = mapped - current
        change = residual - last_residual
        cross_term, square_term = lax.psum(
            (jnp.sum(change * residual), jnp.sum(change * change)), "seq"
        )
        mixing = cross_term / entries / (square_term / entries + mix_eps)
        current = mapped - mixing * (mapped - last_image)
        last_image = mapped
        last_residual = residual
    return current


def solution(mesh):
    in_specs = (
        P("seq", None),
        P("seq", None),
        P(),
        P(None, "head"),
        P(None, "head"),
        P("head", None),
        P("head", "seq"),
        P("seq", "head"),
    )
    out_specs = P("seq", None)
    return jax.shard_map(shards, mesh=mesh, in_specs=in_specs, out_specs=out_specs, check_vma=False)
```

profile of v0, /device:TPU:64, one launch (start us, length us, event | category | flops | bytes accessed | tf_op | source)
XLA Modules:
  0.0 1416.6 jit_solution(17507828075514099444)
XLA Ops:
  7.9 1.6 convolution_convert_fusion.1
  9.5 3.5 collective-permute-start.3
  13.1 5.2 collective-permute-start.2
  18.3 7.0 collective-permute-start.1
  25.3 6.4 collective-permute-start
  45.6 4.4 collective-permute-done.7
  52.2 56.6 %all-reduce.7.cloned.1.call-done = bf16[128,2048]{1,0:T(8,128)(2,1)} async-done(((bf16[128,2048]{1,0:T(8,128)(2,1)}), bf16[128,2048]{1,0:T(8,128)(2,1)}) %all-reduce.7.cloned.1.call-update) | async-done | bytes 524304 | tf_op jit(solution)/shard_map/psum | solution.py:105
  108.8 1.4 fusion.32
  110.3 1.5 fusion.30
  111.7 380.5 %all-reduce.2 = (f32[]{:T(128)}, f32[]{:T(128)}) all-reduce(f32[]{:T(128)} %get-tuple-element.10, f32[]{:T(128)} %get-tuple-element.9), channel_id=1, replica_groups=mesh['seq'=128,'head'=4] {'seq'}, use_global_device_ids=true, to_apply=%region_5.6 | all-reduce | flops 2 | bytes 16 | tf_op jit(solution)/shard_map/psum | solution.py:118
  493.5 2.6 convert_multiply_fusion.9
  496.1 1.6 copy.46
  498.7 1.6 copy.44
  509.1 2.2 collective-permute-done.11
  511.3 1.6 collective-permute-done.10
  512.9 1.6 collective-permute-done.9
  515.7 49.4 %all-reduce.9.cloned.1.call-done = bf16[128,2048]{1,0:T(8,128)(2,1)} async-done(((bf16[128,2048]{1,0:T(8,128)(2,1)}), bf16[128,2048]{1,0:T(8,128)(2,1)}) %all-reduce.9.cloned.1.call-update) | async-done | bytes 524304 | tf_op jit(solution)/shard_map/psum | solution.py:105
  565.1 1.4 fusion.35
  566.5 1.8 multiply_reduce_fusion.2
  568.3 380.5 %all-reduce.1 = (f32[]{:T(128)}, f32[]{:T(128)}) all-reduce(f32[]{:T(128)} %get-tuple-element.8, f32[]{:T(128)} %get-tuple-element.7), channel_id=1, replica_groups=mesh['seq'=128,'head'=4] {'seq'}, use_global_device_ids=true, to_apply=%region_12.13 | all-reduce | flops 2 | bytes 16 | tf_op jit(solution)/shard_map/psum | solution.py:118
  950.1 2.9 convert_multiply_fusion.8
  953.0 1.7 copy.53
  955.6 1.6 copy.51
  964.1 1.5 collective-permute-start.13
  966.1 2.1 collective-permute-done.15
  968.2 1.6 collective-permute-done.14
  969.8 1.6 collective-permute-done.13
  972.5 49.4 %all-reduce.11.cloned.1.call-done = bf16[128,2048]{1,0:T(8,128)(2,1)} async-done(((bf16[128,2048]{1,0:T(8,128)(2,1)}), bf16[128,2048]{1,0:T(8,128)(2,1)}) %all-reduce.11.cloned.1.call-update) | async-done | bytes 524304 | tf_op jit(solution)/shard_map/psum | solution.py:105
  1021.9 1.4 fusion.38
  1023.4 2.1 multiply_reduce_fusion
  1025.5 380.5 %all-reduce = (f32[]{:T(128)}, f32[]{:T(128)}) all-reduce(f32[]{:T(128)} %get-tuple-element.6, f32[]{:T(128)} %get-tuple-element.5), channel_id=1, replica_groups=mesh['seq'=128,'head'=4] {'seq'}, use_global_device_ids=true, to_apply=%region_19.20 | all-reduce | flops 2 | bytes 16 | tf_op jit(solution)/shard_map/psum | solution.py:118
  1407.3 2.8 multiply_subtract_fusion
  (100 shorter events, 37.7 us)
Async XLA Ops:
  6.5 25.7 %copy-start = (bf16[2048,256]{1,0:T(8,128)(2,1)S(1)}, bf16[2048,256]{1,0:T(8,128)(2,1)}, u32[]{:S(2)}) copy-start(bf16[2048,256]{1,0:T(8,128)(2,1)} %param.11) | copy-start | bytes 3145732
  6.5 25.7 %copy-start.1 = (bf16[128,2048]{1,0:T(8,128)(2,1)S(1)}, bf16[128,2048]{1,0:T(8,128)(2,1)}, u32[]{:S(2)}) copy-start(bf16[128,2048]{1,0:T(8,128)(2,1)} %param.8) | copy-start | bytes 1572868
  6.5 25.7 %copy-start.11 = (f32[2048]{0:T(1024)S(1)}, f32[2048]{0:T(1024)}, u32[]{:S(2)}) copy-start(f32[2048]{0:T(1024)} %param.10) | copy-start | bytes 24580
  6.5 102.3 %all-reduce.7.cloned.1.call-start = ((), (), s32[]{:S(2)}) async-start(), calls=%async_computation | async-start | bytes 1048576 | tf_op jit(solution)/shard_map/psum | solution.py:105
  9.5 23.7 %copy-start.2 = (bf16[128,2048]{1,0:T(8,128)(2,1)S(1)}, bf16[128,2048]{1,0:T(8,128)(2,1)}, u32[]{:S(2)}) copy-start(bf16[128,2048]{1,0:T(8,128)(2,1)} %param.9) | copy-start | bytes 1572868
  9.5 23.7 %copy-start.10 = (bf16[256,2048]{1,0:T(8,128)(2,1)S(1)}, bf16[256,2048]{1,0:T(8,128)(2,1)}, u32[]{:S(2)}) copy-start(bf16[256,2048]{1,0:T(8,128)(2,1)} %param.13) | copy-start | bytes 3145732
  9.5 23.7 %copy-start.12 = (bf16[128,256]{1,0:T(8,128)(2,1)S(1)}, bf16[128,256]{1,0:T(8,128)(2,1)}, u32[]{:S(2)}) copy-start(bf16[128,256]{1,0:T(8,128)(2,1)} %param.15) | copy-start | bytes 196612
  9.5 28.5 %collective-permute-start.3 = (bf16[128,128]{1,0:T(8,128)(2,1)S(1)}, bf16[128,128]{1,0:T(8,128)(2,1)S(1)}, u32[]{:S(2)}, u32[]{:S(2)}) collective-permute-start(bf16[128,128]{1,0:T(8,128)(2,1)S(1)} %convolution_convert_fusion.1), channel_id=1, source_target_pairs={{0,4},{4,8},{8,12},{12,16},{16,20},{20,24},{24,28},{28,32},{32,36}... | collective-permute-start | bytes 98312 | tf_op jit(solution)/shard_map/ppermute | solution.py:17
  13.1 24.2 %collective-permute-start.2 = (bf16[128,128]{1,0:T(8,128)(2,1)S(1)}, bf16[128,128]{1,0:T(8,128)(2,1)}, u32[]{:S(2)}, u32[]{:S(2)}) collective-permute-start(bf16[128,128]{1,0:T(8,128)(2,1)S(1)} %convolution_convert_fusion.1), channel_id=1, source_target_pairs={{0,8},{4,12},{8,16},{12,20},{16,24},{20,28},{24,32},{28,36},{32,40... | collective-permute-start | bytes 98312 | tf_op jit(solution)/shard_map/ppermute | solution.py:17
  18.3 18.2 %collective-permute-start.1 = (bf16[128,128]{1,0:T(8,128)(2,1)S(1)}, bf16[128,128]{1,0:T(8,128)(2,1)}, u32[]{:S(2)}, u32[]{:S(2)}) collective-permute-start(bf16[128,128]{1,0:T(8,128)(2,1)S(1)} %convolution_convert_fusion.1), channel_id=1, source_target_pairs={{0,12},{4,16},{8,20},{12,24},{16,28},{20,32},{24,36},{28,40},{32,4... | collective-permute-start | bytes 98312 | tf_op jit(solution)/shard_map/ppermute | solution.py:17
  25.3 10.4 collective-permute-start
  33.7 4.3 copy-start.13
  39.8 5.8 collective-permute-start.4
  41.1 8.9 collective-permute-start.7
  42.4 7.6 collective-permute-start.6
  43.7 7.3 collective-permute-start.5
  45.0 6.0 copy-start.6
  52.2 512.9 %all-reduce.9.cloned.1.call-start = ((), (), s32[]{:S(2)}) async-start(), calls=%async_computation.1 | async-start | bytes 1048576 | tf_op jit(solution)/shard_map/psum | solution.py:105
  108.8 1.5 copy-start.3
  503.3 5.8 collective-permute-start.8
  504.6 6.7 collective-permute-start.11
  505.9 7.0 collective-permute-start.10
  507.2 7.3 collective-permute-start.9
  508.5 6.0 copy-start.7
  515.7 506.3 %all-reduce.11.cloned.1.call-start = ((), (), s32[]{:S(2)}) async-start(), calls=%async_computation.2 | async-start | bytes 1048576 | tf_op jit(solution)/shard_map/psum | solution.py:105
  960.2 5.9 collective-permute-start.12
  961.5 6.7 collective-permute-start.15
  962.8 7.0 collective-permute-start.14
  964.1 7.3 collective-permute-start.13
  965.6 5.8 copy-start.8
  972.5 50.9 %copy-start.5 = (bf16[128,2048]{1,0:T(8,128)(2,1)S(1)}, bf16[128,2048]{1,0:T(8,128)(2,1)}, u32[]{:S(2)}) copy-start(bf16[128,2048]{1,0:T(8,128)(2,1)} %all-reduce.9.cloned.1.call-done) | copy-start | bytes 1572868
  1021.9 1.5 copy-start.9
  (1 other events, 1.5 us)
Sparse Core Ops, SparseCore 0:
  52.3 56.4 all-reduce.6
  515.8 49.2 all-reduce.8
  972.7 49.2 all-reduce.10
where the time goes:
time: 1420 us
  blocking collectives  1140 us (80%)
  waiting for transfers between devices  172 us (12%)
  starting transfers between devices  37.9 us (3%)
  matrix products  20.9 us (1%)
  between operations  17.3 us (1%)
  other arithmetic  17 us (1%)
    psum x3, blocking collectives, shards(): lax.psum((jnp.sum(change * residual), jnp.sum(change * change)), 'seq')  1140 us
    psum x3, waiting for transfers between devices, shards(): lax.psum((partial_value + jnp.dot(grad_keyval, keyval_weight.T, preferred...  155 us
    ppermute x16, starting transfers between devices, shifted(): lax.ppermute(value, axis, [(source, source + steps) for source in range(i...  37.8 us
  transfers between devices with their start and end apart: 19, of which 13 were waited for; matrix products, arithmetic and copies ran while one was open for 1% of the time, Pallas kernels for 0%

commit v1 on v0

v1 whole, which is shorter than its diff:
```python
import functools

import jax
import jax.numpy as jnp
from jax import lax
from jax.experimental import pallas as pl
from jax.experimental.pallas import tpu as pltpu
from jax.sharding import PartitionSpec as P

WIN = 4
ITERS = 3
GROUP = 4
NORM_EPS = 1e-05
MIX_EPS = 1e-06
MESH = pl.DeviceIdType.MESH
BF = jnp.bfloat16
F32 = jnp.float32

NT = (((1,), (1,)), ((), ()))


def dot(a, b, dims=(((1,), (0,)), ((), ()))):
    return lax.dot_general(a, b, dims, preferred_element_type=F32)


def kernel(
    dims,
    entries,
    fp_in,
    up_in,
    gain_ref,
    wq_in,
    wkv_in,
    wo_in,
    ln_ref,
    ao_ref,
    out_ref,
    fp,
    wq,
    wo,
    wkv,
    xs,
    kvwin,
    kt_send,
    kt_recv,
    own_kt,
    hid,
    qpad,
    dopad,
    ktr,
    p_t,
    ds_t,
    ao_t,
    gq,
    normed,
    inv,
    img,
    img_prev,
    w_prev,
    res_prev,
    pq_own,
    pq_other,
    rs1_send,
    rs1_recv,
    rs2_send,
    rs2_recv,
    red_a_send,
    red_a,
    red_b_send,
    red_b,
    red_c_send,
    red_c,
    mix,
    in_sem,
    kv_ssem,
    kv_rsem,
    wkv_ssem,
    wkv_rsem,
    kt_ssem,
    kt_rsem,
    rs_ssem,
    rs_rsem,
    ag_ssem,
    ag_rsem,
    a_ssem,
    a_rsem,
    b_ssem,
    b_rsem,
    c_ssem,
    c_rsem,
):
    nx, nz, ny = dims
    blocks = nx * nz * ny
    rows, width = fp.shape
    part = rows // GROUP
    heads = ln_ref.shape[0]
    edge = qpad.shape[1] // 2
    s = lax.axis_index("seq")
    h = lax.axis_index("head")
    x = lax.rem(s, nx)
    zh = lax.rem(lax.div(s, nx), nz)
    y = lax.div(s, nx * nz)
    zl = lax.div(h, 2)
    c = lax.rem(h, 2)
    sibling = zl * 2 + (1 - c)
    across = (1 - zl) * 2 + c
    mine = pl.ds(pl.multiple_of(h * part, part), part)

    def z_peer(d):
        peer = lax.rem(zh * GROUP + h + d, nz * GROUP)
        return (y * nz + lax.div(peer, GROUP)) * nx + x, lax.rem(peer, GROUP)

    def x_peer(d):
        return (y * nz + zh) * nx + lax.rem(x + d, nx), h

    def y_peer(d):
        return (lax.rem(y + d, ny) * nz + zh) * nx + x, h

    loads = [
        pltpu.make_async_copy(fp_in, fp, in_sem.at[0]),
        pltpu.make_async_copy(wkv_in, wkv.at[h], in_sem.at[1]),
        pltpu.make_async_copy(wq_in, wq, in_sem.at[2]),
        pltpu.make_async_copy(up_in, xs.at[0], in_sem.at[3]),
        pltpu.make_async_copy(wo_in, wo, in_sem.at[4]),
    ]
    for load in loads:
        load.start()

    kvwin[0:WIN] = jnp.zeros((WIN, rows, 2 * edge), BF)
    kt_recv[...] = jnp.zeros(kt_recv.shape, BF)

    barrier = pltpu.get_barrier_semaphore()

    def greet(device):
        pl.semaphore_signal(barrier, inc=1, device_id=device, device_id_type=MESH)

    for o in range(1, WIN + 1):

        @pl.when(s >= o)
        def _(o=o):
            for q in range(GROUP):
                greet((s - o, q))

        @pl.when(s + o < blocks)
        def _(o=o):
            for q in range(GROUP):
                greet((s + o, q))

    for d in range(1, nz * GROUP):
        greet(z_peer(d))
    for d in range(1, nx):
        greet(x_peer(d))
    for d in range(1, ny):
        greet(y_peer(d))
    greeted = (
        GROUP * (jnp.minimum(s, WIN) + jnp.minimum(blocks - 1 - s, WIN))
        + nz * GROUP - 1 + nx - 1 + ny - 1
    )

    gain = gain_ref[...]
    loads[0].wait()
    latent = fp[...].astype(F32)
    inverse = lax.rsqrt(jnp.mean(latent * latent, axis=1, keepdims=True) + NORM_EPS)
    hid[...] = (latent * inverse * gain).astype(BF)
    own_latent = fp[mine, :].astype(F32)
    own_inverse = lax.rsqrt(jnp.mean(own_latent * own_latent, axis=1, keepdims=True) + NORM_EPS)
    inv[...] = jnp.broadcast_to(own_inverse, inv.shape)
    normed[...] = own_latent * own_inverse
    loads[1].wait()
    kvwin[WIN] = dot(hid[...], wkv[h]).astype(BF)

    pl.semaphore_wait(barrier, greeted)

    def kv_copy(o):
        return pltpu.make_async_remote_copy(
            src_ref=kvwin.at[WIN],
            dst_ref=kvwin.at[WIN - o],
            send_sem=kv_ssem.at[o - 1],
            recv_sem=kv_rsem.at[o - 1],
            device_id=(s + o, h),
            device_id_type=MESH,
        )

    for o in range(WIN, 0, -1):

        @pl.when(s + o < blocks)
        def _(o=o):
            kv_copy(o).start()

    def wkv_copy(slot, owner, target):
        return pltpu.make_async_remote_copy(
            src_ref=wkv.at[owner],
            dst_ref=wkv.at[owner],
            send_sem=wkv_ssem.at[slot],
            recv_sem=wkv_rsem.at[slot],
            device_id=(s, target),
            device_id_type=MESH,
        )

    wkv_copy(0, h, sibling).start()
    wkv_copy(1, h, across).start()

    loads[2].wait()
    queries = dot(hid[...], wq[...]).astype(BF)
    zero_half = jnp.zeros((rows, edge), BF)
    for i in range(heads):
        scaled_q = (queries[:, i * edge : (i + 1) * edge].astype(F32) * (edge ** -0.5)).astype(BF)
        qpad[i * rows : (i + 1) * rows, :] = jnp.concatenate([scaled_q, zero_half], axis=1)
    ao_t[...] = ao_ref[...].astype(F32).T
    log_row = jnp.concatenate([ln_ref[i : i + 1, :] for i in range(heads)], axis=1)
    dopad[0:edge, :] = jnp.zeros((edge, heads * rows), BF)
    loads[3].wait()
    base_own = xs[0, mine, :].astype(F32)
    img[...] = base_own
    img_prev[...] = base_own
    res_prev[...] = base_own
    w_prev[...] = jnp.zeros_like(w_prev)
    mix[...] = jnp.zeros_like(mix)
    loads[4].wait()

    key_pos = lax.broadcasted_iota(jnp.int32, (rows, heads * rows), 0)
    query_pos = lax.rem(lax.broadcasted_iota(jnp.int32, (rows, heads * rows), 1), rows)
    for j in range(WIN, -1, -1):
        if j < WIN:

            @pl.when(s >= WIN - j)
            def _(j=j):
                kv_copy(WIN - j).wait_recv()

        block = kvwin[j]
        scores = dot(block, qpad[...], NT)
        weights = jnp.exp(scores - log_row)
        if j == 0:
            weights = jnp.where(key_pos > query_pos, weights, 0.0)
        if j == WIN:
            weights = jnp.where(key_pos <= query_pos, weights, 0.0)
        else:
            weights = jnp.where(s >= WIN - j, weights, 0.0)
        p_t[j] = weights.astype(BF)
        ktr[:, j * rows : (j + 1) * rows] = block.astype(F32).T[0:edge, :].astype(BF)

    def kt_copy(k, o, q):
        return pltpu.make_async_remote_copy(
            src_ref=kt_send.at[k, o, pl.ds(q * part, part), :],
            dst_ref=kt_recv.at[k, o, h],
            send_sem=kt_ssem.at[k, o * GROUP + q],
            recv_sem=kt_rsem.at[k, o * GROUP + h],
            device_id=(s - o, q),
            device_id_type=MESH,
        )

    def kt_arrival(k, o, q):
        return pltpu.make_async_remote_copy(
            src_ref=kt_send.at[k, o, pl.ds(0, part), :],
            dst_ref=kt_recv.at[k, o, q],
            send_sem=kt_ssem.at[k, o * GROUP + q],
            recv_sem=kt_rsem.at[k, o * GROUP + q],
            device_id=(s, q),
            device_id_type=MESH,
        )

    def rs1_copy(k):
        return pltpu.make_async_remote_copy(
            src_ref=rs1_send.at[k],
            dst_ref=rs1_recv.at[k],
            send_sem=rs_ssem.at[k, 0],
            recv_sem=rs_rsem.at[k, 0],
            device_id=(s, sibling),
            device_id_type=MESH,
        )

    def rs2_copy(k):
        return pltpu.make_async_remote_copy(
            src_ref=rs2_send.at[k],
            dst_ref=rs2_recv.at[k],
            send_sem=rs_ssem.at[k, 1],
            recv_sem=rs_rsem.at[k, 1],
            device_id=(s, across),
            device_id_type=MESH,
        )

    def ag_copy(k, slot, owner, target):
        span = pl.ds(pl.multiple_of(owner * part, part), part)
        return pltpu.make_async_remote_copy(
            src_ref=xs.at[k, span, :],
            dst_ref=xs.at[k, span, :],
            send_sem=ag_ssem.at[k - 1, slot],
            recv_sem=ag_rsem.at[k - 1, slot],
            device_id=(s, target),
            device_id_type=MESH,
        )

    def gathered(k):
        ag_copy(k, 1, across, across).wait_recv()
        ag_copy(k, 2, across, sibling).start()
        ag_copy(k, 0, sibling, sibling).wait_recv()
        ag_copy(k, 2, sibling, sibling).wait_recv()

    def red_copy(k, send, recv, ssem, rsem, d, me, peer):
        return pltpu.make_async_remote_copy(
            src_ref=send.at[k],
            dst_ref=recv.at[k, me],
            send_sem=ssem.at[k, d],
            recv_sem=rsem.at[k, d],
            device_id=peer,
            device_id_type=MESH,
        )

    stages = (
        (red_a_send, red_a, a_ssem, a_rsem, nz * GROUP, zh * GROUP + h, z_peer),
        (red_b_send, red_b, b_ssem, b_rsem, nx, x, x_peer),
        (red_c_send, red_c, c_ssem, c_rsem, ny, y, y_peer),
    )

    def red_start(k, stage, value):
        send, recv, ssem, rsem, count, me, peer = stages[stage]
        send[k] = value
        recv[k, me] = value
        for d in range(1, count):
            red_copy(k, send, recv, ssem, rsem, d, me, peer(d)).start()

    def red_finish(k, stage):
        send, recv, ssem, rsem, count, me, peer = stages[stage]
        for d in range(1, count):
            red_copy(k, send, recv, ssem, rsem, d, me, peer(d)).wait_recv()
        total = recv[k, 0]
        for i in range(1, count):
            total = total + recv[k, i]
        return total

    def set_mix(total):
        cross = jnp.sum(total[0:1, :], axis=1, keepdims=True)
        square = jnp.sum(total[1:2, :], axis=1, keepdims=True)
        mixing = cross / entries / (square / entries + MIX_EPS)
        mix[...] = jnp.broadcast_to(mixing, mix.shape)

    def step(k, carry):
        @pl.when(k > 0)
        def _():
            gathered(k)

        grad_out = dot(wo[...], xs[k], NT)
        terms = []
        for i in range(heads):
            piece = grad_out[i * edge : (i + 1) * edge, :]
            terms.append(
                jnp.sum(piece * ao_t[i * edge : (i + 1) * edge, :], axis=0, keepdims=True)
            )
            dopad[edge : 2 * edge, i * rows : (i + 1) * rows] = piece.astype(BF)
        row_terms = jnp.concatenate(terms, axis=1)

        @pl.when(k > 0)
        def _():
            red_start(k - 1, 1, red_finish(k - 1, 0))

        for j in range(WIN + 1):
            o = WIN - j
            probs = p_t[j]
            grad_prob = dot(kvwin[j], dopad[...])
            grad_score = (probs.astype(F32) * (grad_prob - row_terms)).astype(BF)
            ds_t[j * rows : (j + 1) * rows, :] = grad_score
            key_terms = dot(grad_score, qpad[...]) + dot(probs, dopad[...], NT)
            kt_send[k, o] = key_terms.astype(BF)
            if o > 0:

                @pl.when(s >= o)
                def _(o=o):
                    for q in range(GROUP):
                        kt_copy(k, o, q).start()

            else:
                own_kt[...] = key_terms
                for q in range(GROUP):

                    @pl.when(h != q)
                    def _(q=q):
                        kt_copy(k, 0, q).start()

        grad_q = dot(ktr[...], ds_t[...]) * (edge ** -0.5)
        gq[...] = (
            jnp.concatenate([grad_q[:, i * rows : (i + 1) * rows] for i in range(heads)], axis=0)
            .T.astype(BF)
        )

        def quarter(q):
            return gq[pl.ds(pl.multiple_of(q * part, part), part), :]

        theirs = jnp.concatenate([quarter(1 - c), quarter(3 - c)], axis=0)
        rs1_send[k] = dot(theirs, wq[...], NT).astype(BF).reshape(2, part, width)
        rs1_copy(k).start()
        ours = dot(jnp.concatenate([quarter(h), quarter(across)], axis=0), wq[...], NT)
        pq_own[...] = ours[:part]
        rs1_copy(k).wait_recv()
        rs2_send[k] = (ours[part:] + rs1_recv[k, 1 - zl].astype(F32)).astype(BF)
        rs2_copy(k).start()

        @pl.when(k > 0)
        def _():
            red_start(k - 1, 2, red_finish(k - 1, 1))

        @pl.when(k == 0)
        def _():
            wkv_copy(1, across, across).wait_recv()
            wkv_copy(2, across, sibling).start()

        for o in range(WIN + 1):
            for q in range(GROUP):
                if o > 0:

                    @pl.when(s + o < blocks)
                    def _(o=o, q=q):
                        kt_arrival(k, o, q).wait_recv()

                else:

                    @pl.when(h != q)
                    def _(q=q):
                        kt_arrival(k, 0, q).wait_recv()

        own_terms = own_kt[mine, :]
        collected = []
        for q in range(GROUP):
            total = jnp.where(h == q, own_terms, kt_recv[k, 0, q].astype(F32))
            for o in range(1, WIN + 1):
                total = total + kt_recv[k, o, q].astype(F32)
            collected.append(total.astype(BF))

        @pl.when(k == 0)
        def _():
            wkv_copy(0, sibling, sibling).wait_recv()
            wkv_copy(2, sibling, sibling).wait_recv()

        @pl.when(k > 0)
        def _():
            set_mix(red_finish(k - 1, 2))

        hidden_grad = pq_own[...] + rs1_recv[k, zl].astype(F32)
        for q in range(GROUP):
            hidden_grad = hidden_grad + dot(collected[q], wkv[q], NT)
        rs2_copy(k).wait_recv()
        hidden_grad = hidden_grad + rs2_recv[k].astype(F32)
        scaled = hidden_grad * gain_ref[...]
        own_normed = normed[...]
        mapped = inv[:, 0:1] * (
            scaled - own_normed * jnp.mean(scaled * own_normed, axis=1, keepdims=True)
        )
        mixing = mix[0:1, 0:1]
        base = xs[0, mine, :].astype(F32)
        last = img[...]
        current = last - mixing * (last - img_prev[...])
        image = base + (mapped - mixing * (mapped - w_prev[...]))
        xs[k + 1, mine, :] = image.astype(BF)
        ag_copy(k + 1, 1, h, across).start()
        ag_copy(k + 1, 0, h, sibling).start()
        residual = image - current
        change = residual - res_prev[...]

        def lanes(value):
            value = jnp.sum(value, axis=0, keepdims=True)
            total = value[:, 0:128]
            for i in range(1, width // 128):
                total = total + value[:, i * 128 : (i + 1) * 128]
            return total

        sums = jnp.concatenate(
            [lanes(change * residual), lanes(change * change), jnp.zeros((6, 128), F32)], axis=0
        )
        red_start(k, 0, sums)
        img_prev[...] = last
        img[...] = image
        w_prev[...] = mapped
        res_prev[...] = residual
        return carry

    lax.fori_loop(0, ITERS, step, 0)

    last = ITERS - 1
    red_start(last, 1, red_finish(last, 0))
    gathered(ITERS)
    red_start(last, 2, red_finish(last, 1))
    set_mix(red_finish(last, 2))
    final = xs[ITERS].astype(F32)
    out_ref[...] = final - mix[0:1, 0:1] * (final - xs[ITERS - 1].astype(F32))

    for o in range(1, WIN + 1):

        @pl.when(s + o < blocks)
        def _(o=o):
            kv_copy(o).wait_send()

    wkv_copy(0, h, sibling).wait_send()
    wkv_copy(1, h, across).wait_send()
    wkv_copy(2, across, sibling).wait_send()

    def drain(k, carry):
        for o in range(WIN + 1):
            for q in range(GROUP):
                if o > 0:

                    @pl.when(s >= o)
                    def _(o=o, q=q):
                        kt_copy(k, o, q).wait_send()

                else:

                    @pl.when(h != q)
                    def _(q=q):
                        kt_copy(k, 0, q).wait_send()

        rs1_copy(k).wait_send()
        rs2_copy(k).wait_send()
        ag_copy(k + 1, 0, h, sibling).wait_send()
        ag_copy(k + 1, 1, h, across).wait_send()
        ag_copy(k + 1, 2, across, sibling).wait_send()
        for send, recv, ssem, rsem, count, me, peer in stages:
            for d in range(1, count):
                red_copy(k, send, recv, ssem, rsem, d, me, peer(d)).wait_send()
        return carry

    lax.fori_loop(0, ITERS, drain, 0)


def shards(dims, fixed_point, upstream, norm_gain, query_weight, keyval_weight, output_weight, log_norm, attention_out):
    rows, width = fixed_point.shape
    nx, nz, ny = dims
    heads = log_norm.shape[0]
    cols = query_weight.shape[1]
    kv_cols = keyval_weight.shape[1]
    part = rows // GROUP
    keys = (WIN + 1) * rows
    entries = rows * nx * nz * ny * width
    hbm = pl.BlockSpec(memory_space=pl.ANY)
    vmem = pl.BlockSpec(memory_space=pltpu.VMEM)
    dma = pltpu.SemaphoreType.DMA
    state = pltpu.VMEM((part, width), F32)
    scratch = [
        pltpu.VMEM((rows, width), BF),
        pltpu.VMEM((width, cols), BF),
        pltpu.VMEM((cols, width), BF),
        pltpu.VMEM((GROUP, width, kv_cols), BF),
        pltpu.VMEM((ITERS + 1, rows, width), BF),
        pltpu.VMEM((WIN + 1, rows, kv_cols), BF),
        pltpu.VMEM((ITERS, WIN + 1, rows, kv_cols), BF),
        pltpu.VMEM((ITERS, WIN + 1, GROUP, part, kv_cols), BF),
        pltpu.VMEM((rows, kv_cols), F32),
        pltpu.VMEM((rows, width), BF),
        pltpu.VMEM((heads * rows, kv_cols), BF),
        pltpu.VMEM((kv_cols, heads * rows), BF),
        pltpu.VMEM((kv_cols // 2, keys), BF),
        pltpu.VMEM((WIN + 1, rows, heads * rows), BF),
        pltpu.VMEM((keys, heads * rows), BF),
        pltpu.VMEM((cols, rows), F32),
        pltpu.VMEM((rows, cols), BF),
        state,
        pltpu.VMEM((part, 128), F32),
        state,
        state,
        state,
        state,
        state,
        state,
        pltpu.VMEM((ITERS, 2, part, width), BF),
        pltpu.VMEM((ITERS, 2, part, width), BF),
        pltpu.VMEM((ITERS, part, width), BF),
        pltpu.VMEM((ITERS, part, width), BF),
        pltpu.VMEM((ITERS, 8, 128), F32),
        pltpu.VMEM((ITERS, nz * GROUP, 8, 128), F32),
        pltpu.VMEM((ITERS, 8, 128), F32),
        pltpu.VMEM((ITERS, nx, 8, 128), F32),
        pltpu.VMEM((ITERS, 8, 128), F32),
        pltpu.VMEM((ITERS, ny, 8, 128), F32),
        pltpu.VMEM((8, 128), F32),
        dma((5,)),
        dma((WIN,)),
        dma((WIN,)),
        dma((3,)),
        dma((3,)),
        dma((ITERS, (WIN + 1) * GROUP)),
        dma((ITERS, (WIN + 1) * GROUP)),
        dma((ITERS, 2)),
        dma((ITERS, 2)),
        dma((ITERS, 3)),
        dma((ITERS, 3)),
        dma((ITERS, nz * GROUP)),
        dma((ITERS, nz * GROUP)),
        dma((ITERS, nx)),
        dma((ITERS, nx)),
        dma((ITERS, ny)),
        dma((ITERS, ny)),
    ]
    return pl.pallas_call(
        functools.partial(kernel, dims, float(entries)),
        out_shape=jax.ShapeDtypeStruct((rows, width), F32),
        in_specs=[hbm, hbm, vmem, hbm, hbm, hbm, vmem, vmem],
        out_specs=vmem,
        scratch_shapes=scratch,
        compiler_params=pltpu.CompilerParams(
            collective_id=0, has_side_effects=True, vmem_limit_bytes=58 << 20
        ),
        name="adjoint",
    )(
        fixed_point,
        upstream,
        norm_gain.reshape(1, width),
        query_weight,
        keyval_weight,
        output_weight,
        log_norm,
        attention_out,
    )


def solution(mesh, dims=(4, 4, 8)):
    in_specs = (
        P("seq", None),
        P("seq", None),
        P(),
        P(None, "head"),
        P(None, "head"),
        P("head", None),
        P("head", "seq"),
        P("seq", "head"),
    )
    return jax.shard_map(
        functools.partial(shards, dims),
        mesh=mesh,
        in_specs=in_specs,
        out_specs=P("seq", None),
        check_vma=False,
    )
```

time: 1420 us -> 96.4 us (0.07)
  the two profiles are of different devices: /device:TPU:64 before, /device:TPU:1 now
where the time goes in v1:
time: 96.4 us; the launch traced here: 96.2 us
  Pallas kernels  93.9 us (97%)
  local copies, waits for them, and re-layouts  2.3 us (2%)
    pallas_call x1, Pallas kernels, shards(): pl.pallas_call(functools.partial(kernel, dims, float(entries)), out_shape...  93.9 us
    unnamed x1, local copies, waits for them, and re-layouts  2.3 us

profile of v1, /device:TPU:1, one launch (start us, length us, event | category | flops | bytes accessed | tf_op | source)
XLA Modules:
  0.0 96.2 jit_solution(18108028358946975270)
XLA Ops:
  0.0 93.9 %adjoint.1 = f32[128,2048]{1,0:T(8,128)} custom-call(bf16[128,2048]{1,0:T(8,128)(2,1)} %fp_in.1, bf16[128,2048]{1,0:T(8,128)(2,1)} %up_in.1, f32[1,2048]{1,0:T(1,128)} %bitcast.1, bf16[2048,256]{1,0:T(8,128)(2,1)} %wq_in.1, bf16[2048,128]{1,0:T(8,128)(2,1)} %wkv_in.1, bf16[256,2048]{1,0:T(8,128)(2,1)} %wo_in.1, f32[4,128]{1,0:T(4,128)} %ln_ref.1, ...), custom_call_target="tpu_custom_call" | custom-call | tf_op jit(solution)/shard_map/adjoint/pallas_call | solution.py:591
  93.9 2.3 %copy.10 = f32[128,2048]{1,0:T(8,128)} copy(f32[128,2048]{1,0:T(8,128)} %adjoint.1) | data formatting | bytes 2097152

commit v2 on v1

v2 whole, which is shorter than its diff:
```python
import functools

import jax
import jax.numpy as jnp
from jax import lax
from jax.experimental import pallas as pl
from jax.experimental.pallas import tpu as pltpu
from jax.sharding import PartitionSpec as P

WIN = 4
ITERS = 3
GROUP = 4
NORM_EPS = 1e-05
MIX_EPS = 1e-06
MESH = pl.DeviceIdType.MESH
BF = jnp.bfloat16
F32 = jnp.float32

NT = (((1,), (1,)), ((), ()))


def dot(a, b, dims=(((1,), (0,)), ((), ()))):
    return lax.dot_general(a, b, dims, preferred_element_type=F32)


def kernel(
    dims,
    entries,
    fp_in,
    up_in,
    gain_ref,
    wq_in,
    wkv_in,
    wo_in,
    ln_ref,
    ao_ref,
    last_out,
    prev_out,
    mix_out,
    fp,
    wq,
    wo,
    wkv,
    xs,
    kvwin,
    kt_send,
    kt_recv,
    own_kt,
    hid,
    qpad,
    dopad,
    ktr,
    p_t,
    ds_t,
    ao_t,
    gq,
    normed,
    inv,
    img,
    img_prev,
    w_prev,
    res_prev,
    pq_own,
    rs_send,
    rs_recv,
    red_a_send,
    red_a,
    red_b_send,
    red_b,
    red_c_send,
    red_c,
    mix,
    in_sem,
    kv_ssem,
    kv_rsem,
    wkv_ssem,
    wkv_rsem,
    kt_ssem,
    kt_rsem,
    rs_ssem,
    rs_rsem,
    ag_ssem,
    ag_rsem,
    a_ssem,
    a_rsem,
    b_ssem,
    b_rsem,
    c_ssem,
    c_rsem,
):
    nx, nz, ny = dims
    blocks = nx * nz * ny
    rows, width = fp.shape
    part = rows // GROUP
    heads = ln_ref.shape[0]
    edge = qpad.shape[1] // 2
    s = lax.axis_index("seq")
    h = lax.axis_index("head")
    x = lax.rem(s, nx)
    zh = lax.rem(lax.div(s, nx), nz)
    y = lax.div(s, nx * nz)
    zl = lax.div(h, 2)
    c = lax.rem(h, 2)
    sibling = zl * 2 + (1 - c)
    across = (1 - zl) * 2 + c
    mine = pl.ds(pl.multiple_of(h * part, part), part)

    def z_peer(d):
        peer = lax.rem(zh * GROUP + h + d, nz * GROUP)
        return (y * nz + lax.div(peer, GROUP)) * nx + x, lax.rem(peer, GROUP)

    def x_peer(d):
        return (y * nz + zh) * nx + lax.rem(x + d, nx), h

    def y_peer(d):
        return (lax.rem(y + d, ny) * nz + zh) * nx + x, h

    loads = [
        pltpu.make_async_copy(fp_in, fp, in_sem.at[0]),
        pltpu.make_async_copy(wkv_in, wkv.at[h], in_sem.at[1]),
        pltpu.make_async_copy(wq_in, wq.at[c], in_sem.at[2]),
        pltpu.make_async_copy(up_in, xs.at[0], in_sem.at[3]),
        pltpu.make_async_copy(wo_in, wo, in_sem.at[4]),
    ]
    for load in loads:
        load.start()

    kvwin[0:WIN] = jnp.zeros((WIN, rows, 2 * edge), BF)
    kt_recv[...] = jnp.zeros(kt_recv.shape, BF)

    barrier = pltpu.get_barrier_semaphore()

    def greet(device):
        pl.semaphore_signal(barrier, inc=1, device_id=device, device_id_type=MESH)

    for o in range(1, WIN + 1):

        @pl.when(s >= o)
        def _(o=o):
            greet((s - o, h))

        @pl.when(s + o < blocks)
        def _(o=o):
            for q in range(GROUP):
                greet((s + o, q))

    for d in range(1, nz * GROUP):
        greet(z_peer(d))
    for d in range(1, nx):
        greet(x_peer(d))
    for d in range(1, ny):
        greet(y_peer(d))
    greeted = (
        GROUP * jnp.minimum(s, WIN) + jnp.minimum(blocks - 1 - s, WIN)
        + nz * GROUP - 1 + nx - 1 + ny - 1
    )

    gain = gain_ref[...]
    loads[0].wait()
    latent = fp[...].astype(F32)
    inverse = lax.rsqrt(jnp.mean(latent * latent, axis=1, keepdims=True) + NORM_EPS)
    hid[...] = (latent * inverse * gain).astype(BF)
    own_latent = fp[mine, :].astype(F32)
    own_inverse = lax.rsqrt(jnp.mean(own_latent * own_latent, axis=1, keepdims=True) + NORM_EPS)
    inv[...] = jnp.broadcast_to(own_inverse, inv.shape)
    normed[...] = own_latent * own_inverse
    loads[1].wait()
    kvwin[WIN] = dot(hid[...], wkv[h]).astype(BF)

    pl.semaphore_wait(barrier, greeted)

    def kv_copy(o):
        return pltpu.make_async_remote_copy(
            src_ref=kvwin.at[WIN],
            dst_ref=kvwin.at[WIN - o],
            send_sem=kv_ssem.at[o - 1],
            recv_sem=kv_rsem.at[o - 1],
            device_id=(s + o, h),
            device_id_type=MESH,
        )

    for o in range(WIN, 0, -1):

        @pl.when(s + o < blocks)
        def _(o=o):
            kv_copy(o).start()

    def wkv_copy(slot, owner, target):
        return pltpu.make_async_remote_copy(
            src_ref=wkv.at[owner],
            dst_ref=wkv.at[owner],
            send_sem=wkv_ssem.at[slot],
            recv_sem=wkv_rsem.at[slot],
            device_id=(s, target),
            device_id_type=MESH,
        )

    wkv_copy(0, h, sibling).start()
    wkv_copy(1, h, across).start()

    loads[2].wait()

    def wq_copy():
        return pltpu.make_async_remote_copy(
            src_ref=wq.at[c],
            dst_ref=wq.at[c],
            send_sem=wkv_ssem.at[3],
            recv_sem=wkv_rsem.at[3],
            device_id=(s, sibling),
            device_id_type=MESH,
        )

    wq_copy().start()
    queries = dot(hid[...], wq[c]).astype(BF)
    zero_half = jnp.zeros((rows, edge), BF)
    for i in range(heads):
        scaled_q = (queries[:, i * edge : (i + 1) * edge].astype(F32) * (edge ** -0.5)).astype(BF)
        qpad[i * rows : (i + 1) * rows, :] = jnp.concatenate([scaled_q, zero_half], axis=1)
    ao_t[...] = ao_ref[...].astype(F32).T
    log_row = jnp.concatenate([ln_ref[i : i + 1, :] for i in range(heads)], axis=1)
    dopad[0:edge, :] = jnp.zeros((edge, heads * rows), BF)
    loads[3].wait()
    base_own = xs[0, mine, :].astype(F32)
    img[...] = base_own
    img_prev[...] = base_own
    res_prev[...] = base_own
    w_prev[...] = jnp.zeros_like(w_prev)
    mix[...] = jnp.zeros_like(mix)
    loads[4].wait()

    def kt_copy(k, o, q):
        return pltpu.make_async_remote_copy(
            src_ref=kt_send.at[k, o, pl.ds(q * part, part), :],
            dst_ref=kt_recv.at[k, o, h],
            send_sem=kt_ssem.at[k, o * GROUP + q],
            recv_sem=kt_rsem.at[k, o * GROUP + h],
            device_id=(s - o, q),
            device_id_type=MESH,
        )

    def kt_arrival(k, o, q):
        return pltpu.make_async_remote_copy(
            src_ref=kt_send.at[k, o, pl.ds(0, part), :],
            dst_ref=kt_recv.at[k, o, q],
            send_sem=kt_ssem.at[k, o * GROUP + q],
            recv_sem=kt_rsem.at[k, o * GROUP + q],
            device_id=(s, q),
            device_id_type=MESH,
        )

    def gq_copy(k):
        return pltpu.make_async_remote_copy(
            src_ref=gq.at[k, c],
            dst_ref=gq.at[k, c],
            send_sem=rs_ssem.at[k, 0],
            recv_sem=rs_rsem.at[k, 0],
            device_id=(s, sibling),
            device_id_type=MESH,
        )

    def rs_copy(k, n):
        return pltpu.make_async_remote_copy(
            src_ref=rs_send.at[k, n],
            dst_ref=rs_recv.at[k, n],
            send_sem=rs_ssem.at[k, 1 + n],
            recv_sem=rs_rsem.at[k, 1 + n],
            device_id=(s, across),
            device_id_type=MESH,
        )

    def ag_copy(k, slot, owner, target):
        span = pl.ds(pl.multiple_of(owner * part, part), part)
        return pltpu.make_async_remote_copy(
            src_ref=xs.at[k, span, :],
            dst_ref=xs.at[k, span, :],
            send_sem=ag_ssem.at[k - 1, slot],
            recv_sem=ag_rsem.at[k - 1, slot],
            device_id=(s, target),
            device_id_type=MESH,
        )

    def gathered(k):
        ag_copy(k, 1, across, across).wait_recv()
        ag_copy(k, 2, across, sibling).start()
        ag_copy(k, 0, sibling, sibling).wait_recv()
        ag_copy(k, 2, sibling, sibling).wait_recv()

    def red_copy(k, send, recv, ssem, rsem, d, me, peer):
        return pltpu.make_async_remote_copy(
            src_ref=send.at[k],
            dst_ref=recv.at[k, me],
            send_sem=ssem.at[k, d],
            recv_sem=rsem.at[k, d],
            device_id=peer,
            device_id_type=MESH,
        )

    stages = (
        (red_a_send, red_a, a_ssem, a_rsem, nz * GROUP, zh * GROUP + h, z_peer),
        (red_b_send, red_b, b_ssem, b_rsem, nx, x, x_peer),
        (red_c_send, red_c, c_ssem, c_rsem, ny, y, y_peer),
    )

    def red_start(k, stage, value):
        send, recv, ssem, rsem, count, me, peer = stages[stage]
        send[k] = value
        recv[k, me] = value
        for d in range(1, count):
            red_copy(k, send, recv, ssem, rsem, d, me, peer(d)).start()

    def red_finish(k, stage):
        send, recv, ssem, rsem, count, me, peer = stages[stage]
        for d in range(1, count):
            red_copy(k, send, recv, ssem, rsem, d, me, peer(d)).wait_recv()
        total = recv[k, 0]
        for i in range(1, count):
            total = total + recv[k, i]
        return total

    def set_mix(total):
        first = lax.broadcasted_iota(jnp.int32, total.shape, 1) < 64
        cross = jnp.sum(jnp.where(first, total, 0.0), axis=1, keepdims=True)
        square = jnp.sum(jnp.where(first, 0.0, total), axis=1, keepdims=True)
        mixing = cross / entries / (square / entries + MIX_EPS)
        mix[...] = jnp.broadcast_to(mixing, mix.shape)

    key_pos = lax.broadcasted_iota(jnp.int32, (rows, heads * rows), 0)
    query_pos = lax.rem(lax.broadcasted_iota(jnp.int32, (rows, heads * rows), 1), rows)

    def probabilities(j):
        block = kvwin[j]
        weights = jnp.exp(dot(block, qpad[...], NT) - log_row)
        if j == 0:
            weights = jnp.where(key_pos > query_pos, weights, 0.0)
        if j == WIN:
            weights = jnp.where(key_pos <= query_pos, weights, 0.0)
        else:
            weights = jnp.where(s >= WIN - j, weights, 0.0)
        p_t[j] = weights.astype(BF)
        ktr[:, j * rows : (j + 1) * rows] = block.astype(F32).T[0:edge, :].astype(BF)

    def head_cotangents(k):
        grad_out = dot(wo[...], xs[k], NT)
        terms = []
        for i in range(heads):
            piece = grad_out[i * edge : (i + 1) * edge, :]
            terms.append(
                jnp.sum(piece * ao_t[i * edge : (i + 1) * edge, :], axis=0, keepdims=True)
            )
            dopad[edge : 2 * edge, i * rows : (i + 1) * rows] = piece.astype(BF)
        return jnp.concatenate(terms, axis=1)

    def block_terms(k, j, row_terms):
        o = WIN - j
        probs = p_t[j]
        grad_prob = dot(kvwin[j], dopad[...])
        grad_score = (probs.astype(F32) * (grad_prob - row_terms)).astype(BF)
        ds_t[j * rows : (j + 1) * rows, :] = grad_score
        key_terms = dot(grad_score, qpad[...]) + dot(probs, dopad[...], NT)
        kt_send[k, o] = key_terms.astype(BF)
        if o > 0:

            @pl.when(s >= o)
            def _():
                for q in range(GROUP):
                    kt_copy(k, o, q).start()

        else:
            own_kt[...] = key_terms
            for q in range(GROUP):

                @pl.when(h != q)
                def _(q=q):
                    kt_copy(k, 0, q).start()

    def finish(k, first):
        grad_q = dot(ktr[...], ds_t[...]) * (edge ** -0.5)
        gq[k, c] = (
            jnp.concatenate([grad_q[:, i * rows : (i + 1) * rows] for i in range(heads)], axis=0)
            .T.astype(BF)
        )
        gq_copy(k).start()
        if first:
            wkv_copy(1, across, across).wait_recv()
            wkv_copy(2, across, sibling).start()
            wq_copy().wait_recv()
        else:
            red_start(k - 1, 2, red_finish(k - 1, 1))
        gq_copy(k).wait_recv()
        theirs = pl.ds(pl.multiple_of(across * part, part), part)
        for n in range(2):
            half = slice(n * (width // 2), (n + 1) * (width // 2))
            total = jnp.zeros((2 * part, width // 2), F32)
            for i in range(2):
                pair = jnp.concatenate([gq[k, i, theirs, :], gq[k, i, mine, :]], axis=0)
                total = total + dot(pair, wq[i, half, :], NT)
            rs_send[k, n] = total[:part].astype(BF)
            rs_copy(k, n).start()
            pq_own[:, half] = total[part:]

        for o in range(WIN + 1):
            for q in range(GROUP):
                if o > 0:

                    @pl.when(s + o < blocks)
                    def _(o=o, q=q):
                        kt_arrival(k, o, q).wait_recv()

                else:

                    @pl.when(h != q)
                    def _(q=q):
                        kt_arrival(k, 0, q).wait_recv()

        own_terms = own_kt[mine, :]
        collected = []
        for q in range(GROUP):
            total = jnp.where(h == q, own_terms, kt_recv[k, 0, q].astype(F32))
            for o in range(1, WIN + 1):
                total = total + kt_recv[k, o, q].astype(F32)
            collected.append(total.astype(BF))

        if first:
            wkv_copy(0, sibling, sibling).wait_recv()
            wkv_copy(2, sibling, sibling).wait_recv()
        else:
            set_mix(red_finish(k - 1, 2))

        hidden_grad = pq_own[...]
        for q in range(GROUP):
            hidden_grad = hidden_grad + dot(collected[q], wkv[q], NT)
        for n in range(2):
            rs_copy(k, n).wait_recv()
        hidden_grad = hidden_grad + jnp.concatenate(
            [rs_recv[k, 0], rs_recv[k, 1]], axis=1
        ).astype(F32)
        scaled = hidden_grad * gain_ref[...]
        own_normed = normed[...]
        mapped = inv[:, 0:1] * (
            scaled - own_normed * jnp.mean(scaled * own_normed, axis=1, keepdims=True)
        )
        mixing = mix[0:1, 0:1]
        base = xs[0, mine, :].astype(F32)
        last = img[...]
        current = last - mixing * (last - img_prev[...])
        image = base + (mapped - mixing * (mapped - w_prev[...]))
        xs[k + 1, mine, :] = image.astype(BF)
        ag_copy(k + 1, 1, h, across).start()
        ag_copy(k + 1, 0, h, sibling).start()
        residual = image - current
        change = residual - res_prev[...]

        def lanes(value):
            value = jnp.sum(value, axis=0, keepdims=True)
            total = value[:, 0:128]
            for i in range(1, width // 128):
                total = total + value[:, i * 128 : (i + 1) * 128]
            return total

        crosses = lanes(change * residual)
        squares = lanes(change * change)
        first = lax.broadcasted_iota(jnp.int32, crosses.shape, 1) < 64
        sums = jnp.where(
            first, crosses + pltpu.roll(crosses, 64, 1), squares + pltpu.roll(squares, 64, 1)
        )
        red_start(k, 0, sums)
        img_prev[...] = last
        img[...] = image
        w_prev[...] = mapped
        res_prev[...] = residual

    row_terms = head_cotangents(0)
    for j in range(WIN, -1, -1):
        if j < WIN:

            @pl.when(s >= WIN - j)
            def _(j=j):
                kv_copy(WIN - j).wait_recv()

        probabilities(j)
        block_terms(0, j, row_terms)
    finish(0, True)

    def step(k, carry):
        gathered(k)
        row_terms = head_cotangents(k)
        red_start(k - 1, 1, red_finish(k - 1, 0))
        for j in range(WIN + 1):
            block_terms(k, j, row_terms)
        finish(k, False)
        return carry

    lax.fori_loop(1, ITERS, step, 0)


    last = ITERS - 1
    before = pltpu.make_async_copy(xs.at[last], prev_out, in_sem.at[5])
    before.start()
    red_start(last, 1, red_finish(last, 0))
    gathered(ITERS)
    after = pltpu.make_async_copy(xs.at[ITERS], last_out, in_sem.at[6])
    after.start()
    red_start(last, 2, red_finish(last, 1))
    set_mix(red_finish(last, 2))
    mix_out[...] = mix[0:1, 0:1]
    before.wait()
    after.wait()

    for o in range(1, WIN + 1):

        @pl.when(s + o < blocks)
        def _(o=o):
            kv_copy(o).wait_send()

    wkv_copy(0, h, sibling).wait_send()
    wkv_copy(1, h, across).wait_send()
    wkv_copy(2, across, sibling).wait_send()
    wq_copy().wait_send()

    def drain(k, carry):
        for o in range(WIN + 1):
            for q in range(GROUP):
                if o > 0:

                    @pl.when(s >= o)
                    def _(o=o, q=q):
                        kt_copy(k, o, q).wait_send()

                else:

                    @pl.when(h != q)
                    def _(q=q):
                        kt_copy(k, 0, q).wait_send()

        gq_copy(k).wait_send()
        rs_copy(k, 0).wait_send()
        rs_copy(k, 1).wait_send()
        ag_copy(k + 1, 0, h, sibling).wait_send()
        ag_copy(k + 1, 1, h, across).wait_send()
        ag_copy(k + 1, 2, across, sibling).wait_send()
        for send, recv, ssem, rsem, count, me, peer in stages:
            for d in range(1, count):
                red_copy(k, send, recv, ssem, rsem, d, me, peer(d)).wait_send()
        return carry

    lax.fori_loop(0, ITERS, drain, 0)


def shards(dims, fixed_point, upstream, norm_gain, query_weight, keyval_weight, output_weight, log_norm, attention_out):
    rows, width = fixed_point.shape
    nx, nz, ny = dims
    heads = log_norm.shape[0]
    cols = query_weight.shape[1]
    kv_cols = keyval_weight.shape[1]
    part = rows // GROUP
    keys = (WIN + 1) * rows
    entries = rows * nx * nz * ny * width
    hbm = pl.BlockSpec(memory_space=pl.ANY)
    vmem = pl.BlockSpec(memory_space=pltpu.VMEM)
    dma = pltpu.SemaphoreType.DMA
    state = pltpu.VMEM((part, width), F32)
    scratch = [
        pltpu.VMEM((rows, width), BF),
        pltpu.VMEM((2, width, cols), BF),
        pltpu.VMEM((cols, width), BF),
        pltpu.VMEM((GROUP, width, kv_cols), BF),
        pltpu.VMEM((ITERS + 1, rows, width), BF),
        pltpu.VMEM((WIN + 1, rows, kv_cols), BF),
        pltpu.VMEM((ITERS, WIN + 1, rows, kv_cols), BF),
        pltpu.VMEM((ITERS, WIN + 1, GROUP, part, kv_cols), BF),
        pltpu.VMEM((rows, kv_cols), F32),
        pltpu.VMEM((rows, width), BF),
        pltpu.VMEM((heads * rows, kv_cols), BF),
        pltpu.VMEM((kv_cols, heads * rows), BF),
        pltpu.VMEM((kv_cols // 2, keys), BF),
        pltpu.VMEM((WIN + 1, rows, heads * rows), BF),
        pltpu.VMEM((keys, heads * rows), BF),
        pltpu.VMEM((cols, rows), F32),
        pltpu.VMEM((ITERS, 2, rows, cols), BF),
        state,
        pltpu.VMEM((part, 128), F32),
        state,
        state,
        state,
        state,
        state,
        pltpu.VMEM((ITERS, 2, part, width // 2), BF),
        pltpu.VMEM((ITERS, 2, part, width // 2), BF),
        pltpu.VMEM((ITERS, 1, 128), F32),
        pltpu.VMEM((ITERS, nz * GROUP, 1, 128), F32),
        pltpu.VMEM((ITERS, 1, 128), F32),
        pltpu.VMEM((ITERS, nx, 1, 128), F32),
        pltpu.VMEM((ITERS, 1, 128), F32),
        pltpu.VMEM((ITERS, ny, 1, 128), F32),
        pltpu.VMEM((8, 128), F32),
        dma((7,)),
        dma((WIN,)),
        dma((WIN,)),
        dma((4,)),
        dma((4,)),
        dma((ITERS, (WIN + 1) * GROUP)),
        dma((ITERS, (WIN + 1) * GROUP)),
        dma((ITERS, 3)),
        dma((ITERS, 3)),
        dma((ITERS, 3)),
        dma((ITERS, 3)),
        dma((ITERS, nz * GROUP)),
        dma((ITERS, nz * GROUP)),
        dma((ITERS, nx)),
        dma((ITERS, nx)),
        dma((ITERS, ny)),
        dma((ITERS, ny)),
    ]
    last_image, previous, mixing = pl.pallas_call(
        functools.partial(kernel, dims, float(entries)),
        out_shape=(
            jax.ShapeDtypeStruct((rows, width), BF),
            jax.ShapeDtypeStruct((rows, width), BF),
            jax.ShapeDtypeStruct((1, 1), F32),
        ),
        in_specs=[hbm, hbm, vmem, hbm, hbm, hbm, vmem, vmem],
        out_specs=(hbm, hbm, vmem),
        scratch_shapes=scratch,
        compiler_params=pltpu.CompilerParams(
            collective_id=0, has_side_effects=True, vmem_limit_bytes=58 << 20
        ),
        name="adjoint",
    )(
        fixed_point,
        upstream,
        norm_gain.reshape(1, width),
        query_weight,
        keyval_weight,
        output_weight,
        log_norm,
        attention_out,
    )
    image = last_image.astype(F32)
    return image - mixing * (image - previous.astype(F32))


def solution(mesh, dims=(4, 4, 8)):
    in_specs = (
        P("seq", None),
        P("seq", None),
        P(),
        P(None, "head"),
        P(None, "head"),
        P("head", None),
        P("head", "seq"),
        P("seq", "head"),
    )
    return jax.shard_map(
        functools.partial(shards, dims),
        mesh=mesh,
        in_specs=in_specs,
        out_specs=P("seq", None),
        check_vma=False,
    )
```

time: 96.4 us -> 95.1 us (0.987)
  other arithmetic: 0 us -> 2.91 us
  local copies, waits for them, and re-layouts: 2.3 us -> 0 us
  Pallas kernels: 93.9 us -> 91.7 us
    sub x0 -> x1, other arithmetic: none -> 2.91 us  [shards(): return image - mixing * (image - previous.astype(F32))]
    unnamed x1 -> x0, local copies, waits for them, and re-layouts: 2.3 us -> none
    pallas_call x1, Pallas kernels: 93.9 us -> 91.7 us  [shards(): pl.pallas_call(functools.partial(kernel, dims, float(entries)), out_shape...]
where the time goes in v2:
time: 95.1 us; the launch traced here: 94.6 us
  Pallas kernels  91.7 us (96%)
  other arithmetic  2.91 us (3%)
    pallas_call x1, Pallas kernels, shards(): pl.pallas_call(functools.partial(kernel, dims, float(entries)), out_shape...  91.7 us
    sub x1, other arithmetic, shards(): return image - mixing * (image - previous.astype(F32))  2.91 us

profile of v2, /device:TPU:1, one launch (start us, length us, event | category | flops | bytes accessed | tf_op | source)
XLA Modules:
  0.0 94.6 jit_solution(7706343321854554199)
XLA Ops:
  0.0 91.7 %adjoint.1 = (bf16[128,2048]{1,0:T(8,128)(2,1)}, bf16[128,2048]{1,0:T(8,128)(2,1)}, f32[1,1]{1,0:T(1,128)}) custom-call(bf16[128,2048]{1,0:T(8,128)(2,1)} %fp_in.1, bf16[128,2048]{1,0:T(8,128)(2,1)} %up_in.1, f32[1,2048]{1,0:T(1,128)} %bitcast.2, bf16[2048,256]{1,0:T(8,128)(2,1)} %wq_in.1, bf16[2048,128]{1,0:T(8,128)(2,1)} %wkv_in.1, ...), custom_call_target="tpu_custom_call" | custom-call | tf_op jit(solution)/shard_map/adjoint/pallas_call | solution.py:614
  91.7 2.9 %convert_subtract_fusion = f32[128,2048]{1,0:T(8,128)} fusion(bf16[128,2048]{1,0:T(8,128)(2,1)} %get-tuple-element.8, bf16[128,2048]{1,0:T(8,128)(2,1)} %get-tuple-element.10, f32[]{:T(128)} %bitcast.1), kind=kLoop, calls=%fused_computation | loop fusion | flops 1310720 | bytes 2097156 | tf_op jit(solution)/shard_map/sub | solution.py:639

commit v3 on v2

v3 whole, which is shorter than its diff:
```python
import functools

import jax
import jax.numpy as jnp
from jax import lax
from jax.experimental import pallas as pl
from jax.experimental.pallas import tpu as pltpu
from jax.sharding import PartitionSpec as P

WIN = 4
ITERS = 3
GROUP = 4
NORM_EPS = 1e-05
SCALE = 2.0**-12
RESCALE = SCALE**-2
PAIRS = [(i, j) for j in range(ITERS + 1) for i in range(j + 1)]
MIX_EPS = 1e-06
MESH = pl.DeviceIdType.MESH
BF = jnp.bfloat16
F32 = jnp.float32

NT = (((1,), (1,)), ((), ()))


def dot(a, b, dims=(((1,), (0,)), ((), ()))):
    return lax.dot_general(a, b, dims, preferred_element_type=F32)


def kernel(
    dims,
    entries,
    fp_in,
    up_in,
    gain_ref,
    wq_in,
    wkv_in,
    wo_in,
    ln_ref,
    ao_ref,
    xs_out,
    factor_1,
    factor_2,
    factor_3,
    fp,
    wq,
    wo,
    wkv,
    xs,
    kvwin,
    kt_send,
    kt_recv,
    own_kt,
    hid,
    qd,
    dopad,
    ktr,
    sp,
    ao_t,
    gq,
    normed,
    inv,
    krylov,
    pq_own,
    rs_send,
    rs_recv,
    red_a_send,
    red_a,
    red_b_send,
    red_b,
    red_c_send,
    red_c,
    gram,
    in_sem,
    kv_ssem,
    kv_rsem,
    wkv_ssem,
    wkv_rsem,
    kt_ssem,
    kt_rsem,
    rs_ssem,
    rs_rsem,
    ag_ssem,
    ag_rsem,
    red_ssem,
    red_rsem,
):
    factor_outs = (factor_1, factor_2, factor_3)
    nx, nz, ny = dims
    blocks = nx * nz * ny
    rows, width = fp.shape
    part = rows // GROUP
    heads = ln_ref.shape[0]
    edge = qd.shape[1] // 2
    span = heads * rows
    s = lax.axis_index("seq")
    h = lax.axis_index("head")
    x = lax.rem(s, nx)
    zh = lax.rem(lax.div(s, nx), nz)
    y = lax.div(s, nx * nz)
    zl = lax.div(h, 2)
    c = lax.rem(h, 2)
    sibling = zl * 2 + (1 - c)
    across = (1 - zl) * 2 + c
    mine = pl.ds(pl.multiple_of(h * part, part), part)

    def z_peer(d):
        peer = lax.rem(zh * GROUP + h + d, nz * GROUP)
        return (y * nz + lax.div(peer, GROUP)) * nx + x, lax.rem(peer, GROUP)

    def x_peer(d):
        return (y * nz + zh) * nx + lax.rem(x + d, nx), h

    def y_peer(d):
        return (lax.rem(y + d, ny) * nz + zh) * nx + x, h

    def wkv_of(owner):
        lanes = pl.ds(pl.multiple_of(lax.rem(owner, 2) * 2 * edge, 2 * edge), 2 * edge)
        return wkv.at[lax.div(owner, 2), :, lanes]

    loads = [
        pltpu.make_async_copy(fp_in, fp, in_sem.at[0]),
        pltpu.make_async_copy(wkv_in, wkv_of(h), in_sem.at[1]),
        pltpu.make_async_copy(wq_in, wq.at[c], in_sem.at[2]),
        pltpu.make_async_copy(up_in, xs.at[0], in_sem.at[3]),
        pltpu.make_async_copy(wo_in, wo, in_sem.at[4]),
    ]
    for load in loads:
        load.start()

    kvwin[0:WIN] = jnp.zeros((WIN, rows, 2 * edge), BF)
    kt_recv[...] = jnp.zeros(kt_recv.shape, BF)

    barrier = pltpu.get_barrier_semaphore()

    def greet(device):
        pl.semaphore_signal(barrier, inc=1, device_id=device, device_id_type=MESH)

    for o in range(1, WIN + 1):

        @pl.when(s >= o)
        def _(o=o):
            greet((s - o, h))

        @pl.when(s + o < blocks)
        def _(o=o):
            for q in range(GROUP):
                greet((s + o, q))

    for d in range(1, nz * GROUP):
        greet(z_peer(d))
    for d in range(1, nx):
        greet(x_peer(d))
    for d in range(1, ny):
        greet(y_peer(d))
    greeted = (
        GROUP * jnp.minimum(s, WIN) + jnp.minimum(blocks - 1 - s, WIN)
        + nz * GROUP - 1 + nx - 1 + ny - 1
    )

    gain = gain_ref[...]
    loads[0].wait()
    latent = fp[...].astype(F32)
    inverse = lax.rsqrt(jnp.mean(latent * latent, axis=1, keepdims=True) + NORM_EPS)
    hid[...] = (latent * inverse * gain).astype(BF)
    own_latent = fp[mine, :].astype(F32)
    own_inverse = lax.rsqrt(jnp.mean(own_latent * own_latent, axis=1, keepdims=True) + NORM_EPS)
    inv[...] = jnp.broadcast_to(own_inverse, inv.shape)
    normed[...] = own_latent * own_inverse
    loads[1].wait()
    kvwin[WIN] = dot(hid[...], wkv_of(h)[...]).astype(BF)

    pl.semaphore_wait(barrier, greeted)

    def kv_copy(o):
        return pltpu.make_async_remote_copy(
            src_ref=kvwin.at[WIN],
            dst_ref=kvwin.at[WIN - o],
            send_sem=kv_ssem.at[o - 1],
            recv_sem=kv_rsem.at[o - 1],
            device_id=(s + o, h),
            device_id_type=MESH,
        )

    for o in range(WIN, 0, -1):

        @pl.when(s + o < blocks)
        def _(o=o):
            kv_copy(o).start()

    def wkv_copy(slot, owner, target):
        return pltpu.make_async_remote_copy(
            src_ref=wkv_of(owner),
            dst_ref=wkv_of(owner),
            send_sem=wkv_ssem.at[slot],
            recv_sem=wkv_rsem.at[slot],
            device_id=(s, target),
            device_id_type=MESH,
        )

    wkv_copy(0, h, sibling).start()
    wkv_copy(1, h, across).start()

    loads[2].wait()

    def wq_copy():
        return pltpu.make_async_remote_copy(
            src_ref=wq.at[c],
            dst_ref=wq.at[c],
            send_sem=wkv_ssem.at[3],
            recv_sem=wkv_rsem.at[3],
            device_id=(s, sibling),
            device_id_type=MESH,
        )

    wq_copy().start()
    queries = dot(hid[...], wq[c]).astype(BF)
    zero_half = jnp.zeros((rows, edge), BF)
    for i in range(heads):
        scaled_q = (queries[:, i * edge : (i + 1) * edge].astype(F32) * (edge ** -0.5)).astype(BF)
        qd[i * rows : (i + 1) * rows, :] = jnp.concatenate([scaled_q, zero_half], axis=1)
    ao_t[...] = ao_ref[...].astype(F32).T
    log_row = jnp.concatenate([ln_ref[i : i + 1, :] for i in range(heads)], axis=1)
    dopad[0:edge, :] = jnp.zeros((edge, span), BF)
    qd[span:, 0:edge] = jnp.zeros((span, edge), BF)
    loads[3].wait()
    base_own = xs[0, mine, :].astype(F32)
    krylov[0] = base_own
    krylov[1:ITERS] = jnp.zeros((ITERS - 1,) + base_own.shape, F32)
    loads[4].wait()

    def kt_copy(k, o, q):
        return pltpu.make_async_remote_copy(
            src_ref=kt_send.at[k, WIN - o, pl.ds(q * part, part), :],
            dst_ref=kt_recv.at[k, o, h],
            send_sem=kt_ssem.at[k, o],
            recv_sem=kt_rsem.at[k, o],
            device_id=(s - o, q),
            device_id_type=MESH,
        )

    def kt_all(k, o):
        count = GROUP if o > 0 else GROUP - 1
        return pltpu.make_async_remote_copy(
            src_ref=kt_recv.at[k, o, pl.ds(0, count)],
            dst_ref=kt_recv.at[k, o, pl.ds(0, count)],
            send_sem=kt_ssem.at[k, o],
            recv_sem=kt_rsem.at[k, o],
            device_id=(s, sibling),
            device_id_type=MESH,
        )

    def gq_copy(k):
        return pltpu.make_async_remote_copy(
            src_ref=gq.at[k, c],
            dst_ref=gq.at[k, c],
            send_sem=rs_ssem.at[k, 0],
            recv_sem=rs_rsem.at[k, 0],
            device_id=(s, sibling),
            device_id_type=MESH,
        )

    def rs_copy(k, n):
        return pltpu.make_async_remote_copy(
            src_ref=rs_send.at[k, n],
            dst_ref=rs_recv.at[k, n],
            send_sem=rs_ssem.at[k, 1 + n],
            recv_sem=rs_rsem.at[k, 1 + n],
            device_id=(s, across),
            device_id_type=MESH,
        )

    def ag_copy(k, slot, owner, target):
        span = pl.ds(pl.multiple_of(owner * part, part), part)
        return pltpu.make_async_remote_copy(
            src_ref=xs.at[k, span, :],
            dst_ref=xs.at[k, span, :],
            send_sem=ag_ssem.at[k - 1, slot],
            recv_sem=ag_rsem.at[k - 1, slot],
            device_id=(s, target),
            device_id_type=MESH,
        )

    def gathered(k):
        ag_copy(k, 1, across, across).wait_recv()
        ag_copy(k, 2, across, sibling).start()
        ag_copy(k, 0, sibling, sibling).wait_recv()
        ag_copy(k, 2, sibling, sibling).wait_recv()

    stages = (
        (red_a_send, red_a, nz * GROUP, zh * GROUP + h, z_peer),
        (red_b_send, red_b, nx, x, x_peer),
        (red_c_send, red_c, ny, y, y_peer),
    )

    def red_all(stage):
        send, recv, count, me, peer = stages[stage]
        return pltpu.make_async_remote_copy(
            src_ref=recv.at[pl.ds(0, count - 1)],
            dst_ref=recv.at[pl.ds(0, count - 1)],
            send_sem=red_ssem.at[stage],
            recv_sem=red_rsem.at[stage],
            device_id=peer(1),
            device_id_type=MESH,
        )

    def red_start(stage, value):
        send, recv, count, me, peer = stages[stage]
        send[...] = value
        recv[me] = value
        for d in range(1, count):
            pltpu.make_async_remote_copy(
                src_ref=send,
                dst_ref=recv.at[me],
                send_sem=red_ssem.at[stage],
                recv_sem=red_rsem.at[stage],
                device_id=peer(d),
                device_id_type=MESH,
            ).start()

    def red_finish(stage):
        send, recv, count, me, peer = stages[stage]
        red_all(stage).wait_recv()
        total = recv[0]
        for i in range(1, count):
            total = total + recv[i]
        return total

    group_of_lane = lax.div(lax.broadcasted_iota(jnp.int32, (16, 128), 1), 8)
    row_of = lax.broadcasted_iota(jnp.int32, (16, 128), 0)

    def packed(sums):
        for shift in (64, 32, 16, 8):
            sums = sums + pltpu.roll(sums, shift, 1)
        return jnp.sum(jnp.where(group_of_lane == row_of, sums, 0.0), axis=0, keepdims=True)

    def coefficients(total):
        spread = jnp.where(group_of_lane == row_of, jnp.broadcast_to(total, (16, 128)), 0.0)
        column = jnp.sum(spread, axis=1, keepdims=True)
        index = {pair: i for i, pair in enumerate(PAIRS)}

        def inner(a, b):
            value = 0.0
            for i, left in enumerate(a):
                for j, right in enumerate(b):
                    if left is not None and right is not None:
                        at = index[min(i, j), max(i, j)]
                        value = value + left * right * column[at : at + 1, :]
            return value

        def combined(a, b, factor):
            out = []
            for left, right in zip(a, b):
                if right is None:
                    out.append(left)
                else:
                    out.append(factor * right if left is None else left + factor * right)
            return out

        one = jnp.ones((1, 1), F32)
        base = [one] + [None] * ITERS
        last_image, last_residual, current = base, base, base
        for _ in range(ITERS):
            image = combined(base, [None] + current[:ITERS], 1.0)
            residual = combined(image, current, -1.0)
            change = combined(residual, last_residual, -1.0)
            cross = inner(change, residual) * (RESCALE / entries)
            square = inner(change, change) * (RESCALE / entries)
            mixing = cross / (square + MIX_EPS)
            current = combined(image, combined(image, last_image, -1.0), -mixing)
            last_image, last_residual = image, residual
        return current

    key_pos = lax.broadcasted_iota(jnp.int32, (rows, span), 0)
    query_pos = lax.rem(lax.broadcasted_iota(jnp.int32, (rows, span), 1), rows)

    def probabilities(j):
        block = kvwin[j]
        weights = jnp.exp(dot(block, qd[0:span, :], NT) - log_row)
        if j == 0:
            weights = jnp.where(key_pos > query_pos, weights, 0.0)
        if j == WIN:
            weights = jnp.where(key_pos <= query_pos, weights, 0.0)
        else:
            weights = jnp.where(s >= WIN - j, weights, 0.0)
        sp[j * rows : (j + 1) * rows, span:] = weights.astype(BF)
        ktr[:, j * rows : (j + 1) * rows] = block.astype(F32).T[0:edge, :].astype(BF)

    def head_cotangents(k):
        grad_out = dot(wo[...], xs[k], NT)
        terms = []
        for i in range(heads):
            piece = grad_out[i * edge : (i + 1) * edge, :]
            terms.append(
                jnp.sum(piece * ao_t[i * edge : (i + 1) * edge, :], axis=0, keepdims=True)
            )
            dopad[edge : 2 * edge, i * rows : (i + 1) * rows] = piece.astype(BF)
            qd[span + i * rows : span + (i + 1) * rows, edge:] = piece.T.astype(BF)
        return jnp.concatenate(terms, axis=1)

    def block_terms(k, low, high, row_terms):
        count = high - low
        keys = slice(low * rows, high * rows)
        grad_prob = dot(kvwin[low:high].reshape(count * rows, 2 * edge), dopad[...])
        probs = sp[keys, span:]
        sp[keys, :span] = (probs.astype(F32) * (grad_prob - row_terms)).astype(BF)
        key_terms = dot(sp[keys, :], qd[...])
        kt_send[k, low:high] = key_terms.astype(BF).reshape(count, rows, 2 * edge)
        if high == WIN + 1:
            own_kt[...] = key_terms[(count - 1) * rows :]
        for j in range(low, high):
            o = WIN - j
            if o > 0:

                @pl.when(s >= o)
                def _(o=o):
                    for q in range(GROUP):
                        kt_copy(k, o, q).start()

            else:
                for q in range(GROUP):

                    @pl.when(h != q)
                    def _(q=q):
                        kt_copy(k, 0, q).start()

    def lanes(value):
        value = jnp.sum(value, axis=0, keepdims=True)
        total = value[:, 0:128]
        for i in range(1, width // 128):
            total = total + value[:, i * 128 : (i + 1) * 128]
        return total

    def add_inner(newest, count):
        right = krylov[newest] * SCALE
        row = lax.div(newest * (newest + 1), 2)
        for i in range(count):
            gram[pl.ds(row + i, 1), :] = lanes(krylov[i] * SCALE * right)

    def finish(k, first):
        grad_q = dot(ktr[...], sp[:, :span]) * (edge ** -0.5)
        gq[k, c] = (
            jnp.concatenate([grad_q[:, i * rows : (i + 1) * rows] for i in range(heads)], axis=0)
            .T.astype(BF)
        )
        gq_copy(k).start()
        add_inner(jnp.int32(k), ITERS)
        if first:
            wkv_copy(1, across, across).wait_recv()
            wkv_copy(2, across, sibling).start()
            wq_copy().wait_recv()
        gq_copy(k).wait_recv()
        theirs = pl.ds(pl.multiple_of(across * part, part), part)
        for n in range(2):
            half = slice(n * (width // 2), (n + 1) * (width // 2))
            total = jnp.zeros((2 * part, width // 2), F32)
            for i in range(2):
                pair = jnp.concatenate([gq[k, i, theirs, :], gq[k, i, mine, :]], axis=0)
                total = total + dot(pair, wq[i, half, :], NT)
            rs_send[k, n] = total[:part].astype(BF)
            rs_copy(k, n).start()
            pq_own[:, half] = total[part:]

        for o in range(1, WIN + 1):

            @pl.when(s + o < blocks)
            def _(o=o):
                kt_all(k, o).wait_recv()

        kt_all(k, 0).wait_recv()
        own_terms = own_kt[mine, :]
        collected = []
        for q in range(GROUP):
            total = jnp.where(h == q, own_terms, kt_recv[k, 0, q].astype(F32))
            for o in range(1, WIN + 1):
                total = total + kt_recv[k, o, q].astype(F32)
            collected.append(total.astype(BF))

        if first:
            wkv_copy(0, sibling, sibling).wait_recv()
            wkv_copy(2, sibling, sibling).wait_recv()

        hidden_grad = pq_own[...]
        for i in range(2):
            pair = jnp.concatenate(collected[2 * i : 2 * i + 2], axis=1)
            hidden_grad = hidden_grad + dot(pair, wkv[i], NT)
        for n in range(2):
            rs_copy(k, n).wait_recv()
        hidden_grad = hidden_grad + jnp.concatenate(
            [rs_recv[k, 0], rs_recv[k, 1]], axis=1
        ).astype(F32)
        scaled = hidden_grad * gain_ref[...]
        own_normed = normed[...]
        mapped = inv[:, 0:1] * (
            scaled - own_normed * jnp.mean(scaled * own_normed, axis=1, keepdims=True)
        )
        xs[k + 1, mine, :] = mapped.astype(BF)
        ag_copy(k + 1, 1, h, across).start()
        ag_copy(k + 1, 0, h, sibling).start()
        krylov[k + 1] = mapped

    row_terms = head_cotangents(0)
    for j in range(WIN, -1, -1):
        if j < WIN:

            @pl.when(s >= WIN - j)
            def _(j=j):
                kv_copy(WIN - j).wait_recv()

        probabilities(j)
        block_terms(0, j, j + 1, row_terms)
    gram[...] = jnp.zeros_like(gram)
    finish(0, True)

    def step(k, carry):
        gathered(k)
        block_terms(k, 0, WIN + 1, head_cotangents(k))
        finish(k, False)
        return carry

    lax.fori_loop(1, ITERS, step, 0)

    add_inner(jnp.int32(ITERS), ITERS + 1)
    red_start(0, packed(gram[...]))
    total = red_finish(0)
    red_start(1, total)
    gathered(ITERS)
    kept = pltpu.make_async_copy(xs.at[pl.ds(1, ITERS)], xs_out, in_sem.at[5])
    kept.start()
    total = red_finish(1)
    red_start(2, total)
    factors = coefficients(red_finish(2))
    for i in range(ITERS):
        factor_outs[i][...] = factors[i + 1]
    kept.wait()

    for o in range(1, WIN + 1):

        @pl.when(s + o < blocks)
        def _(o=o):
            kv_copy(o).wait_send()

    wkv_copy(0, h, sibling).wait_send()
    wkv_copy(1, h, across).wait_send()
    wkv_copy(2, across, sibling).wait_send()
    wq_copy().wait_send()

    for stage in range(3):
        red_all(stage).wait_send()

    def drain(k, carry):
        for o in range(1, WIN + 1):

            @pl.when(s >= o)
            def _(o=o):
                kt_all(k, o).wait_send()

        kt_all(k, 0).wait_send()
        gq_copy(k).wait_send()
        rs_copy(k, 0).wait_send()
        rs_copy(k, 1).wait_send()
        ag_copy(k + 1, 0, h, sibling).wait_send()
        ag_copy(k + 1, 1, h, across).wait_send()
        ag_copy(k + 1, 2, across, sibling).wait_send()
        return carry

    lax.fori_loop(0, ITERS, drain, 0)


def shards(dims, fixed_point, upstream, norm_gain, query_weight, keyval_weight, output_weight, log_norm, attention_out):
    rows, width = fixed_point.shape
    nx, nz, ny = dims
    heads = log_norm.shape[0]
    cols = query_weight.shape[1]
    kv_cols = keyval_weight.shape[1]
    part = rows // GROUP
    keys = (WIN + 1) * rows
    entries = rows * nx * nz * ny * width
    hbm = pl.BlockSpec(memory_space=pl.ANY)
    vmem = pl.BlockSpec(memory_space=pltpu.VMEM)
    dma = pltpu.SemaphoreType.DMA
    state = pltpu.VMEM((part, width), F32)
    scratch = [
        pltpu.VMEM((rows, width), BF),
        pltpu.VMEM((2, width, cols), BF),
        pltpu.VMEM((cols, width), BF),
        pltpu.VMEM((2, width, 2 * kv_cols), BF),
        pltpu.VMEM((ITERS + 1, rows, width), BF),
        pltpu.VMEM((WIN + 1, rows, kv_cols), BF),
        pltpu.VMEM((ITERS, WIN + 1, rows, kv_cols), BF),
        pltpu.VMEM((ITERS, WIN + 1, GROUP, part, kv_cols), BF),
        pltpu.VMEM((rows, kv_cols), F32),
        pltpu.VMEM((rows, width), BF),
        pltpu.VMEM((2 * heads * rows, kv_cols), BF),
        pltpu.VMEM((kv_cols, heads * rows), BF),
        pltpu.VMEM((kv_cols // 2, keys), BF),
        pltpu.VMEM((keys, 2 * heads * rows), BF),
        pltpu.VMEM((cols, rows), F32),
        pltpu.VMEM((ITERS, 2, rows, cols), BF),
        state,
        pltpu.VMEM((part, 128), F32),
        pltpu.VMEM((ITERS + 1, part, width), F32),
        state,
        pltpu.VMEM((ITERS, 2, part, width // 2), BF),
        pltpu.VMEM((ITERS, 2, part, width // 2), BF),
        pltpu.VMEM((1, 128), F32),
        pltpu.VMEM((nz * GROUP, 1, 128), F32),
        pltpu.VMEM((1, 128), F32),
        pltpu.VMEM((nx, 1, 128), F32),
        pltpu.VMEM((1, 128), F32),
        pltpu.VMEM((ny, 1, 128), F32),
        pltpu.VMEM((16, 128), F32),
        dma((7,)),
        dma((WIN,)),
        dma((WIN,)),
        dma((4,)),
        dma((4,)),
        dma((ITERS, WIN + 1)),
        dma((ITERS, WIN + 1)),
        dma((ITERS, 3)),
        dma((ITERS, 3)),
        dma((ITERS, 3)),
        dma((ITERS, 3)),
        dma((3,)),
        dma((3,)),
    ]
    images, *factors = pl.pallas_call(
        functools.partial(kernel, dims, float(entries)),
        out_shape=(
            pltpu.VMEM((ITERS, rows, width), BF),
        )
        + (jax.ShapeDtypeStruct((1, 1), F32),) * ITERS,
        in_specs=[hbm, hbm, vmem, hbm, hbm, hbm, vmem, vmem],
        out_specs=(vmem,) + (vmem,) * ITERS,
        scratch_shapes=scratch,
        compiler_params=pltpu.CompilerParams(
            collective_id=0, has_side_effects=True, vmem_limit_bytes=58 << 20
        ),
        name="adjoint",
    )(
        fixed_point,
        upstream,
        norm_gain.reshape(1, width),
        query_weight,
        keyval_weight,
        output_weight,
        log_norm,
        attention_out,
    )
    total = upstream.astype(F32)
    for i in range(ITERS):
        total = total + factors[i] * images[i].astype(F32)
    return total


def solution(mesh, dims=(4, 4, 8)):
    in_specs = (
        P("seq", None),
        P("seq", None),
        P(),
        P(None, "head"),
        P(None, "head"),
        P("head", None),
        P("head", "seq"),
        P("seq", "head"),
    )
    return jax.shard_map(
        functools.partial(shards, dims),
        mesh=mesh,
        in_specs=in_specs,
        out_specs=P("seq", None),
        check_vma=False,
    )
```

time: 95.1 us -> 91.4 us (0.961)
  Pallas kernels: 91.7 us -> 87.5 us
    pallas_call x1, Pallas kernels: 91.7 us -> 87.5 us  [shards(): pl.pallas_call(functools.partial(kernel, dims, float(entries)), out_shape...]
    add x0 -> x1, other arithmetic: none -> 3.2 us  [shards(): total = total + factors[i] * images[i].astype(F32)]
    sub x1 -> x0, other arithmetic: 2.91 us -> none  [shards(): return image - mixing * (image - previous.astype(F32))]
where the time goes in v3:
time: 91.4 us; the launch traced here: 90.7 us
  Pallas kernels  87.5 us (96%)
  other arithmetic  3.2 us (4%)
    pallas_call x1, Pallas kernels, shards(): pl.pallas_call(functools.partial(kernel, dims, float(entries)), out_shape...  87.5 us
    add x1, other arithmetic, shards(): total = total + factors[i] * images[i].astype(F32)  3.2 us

profile of v3, /device:TPU:1, one launch (start us, length us, event | category | flops | bytes accessed | tf_op | source)
XLA Modules:
  0.0 90.7 jit_solution(16614880119926663504)
XLA Ops:
  0.0 0.0 copy-start
  0.0 87.5 %adjoint.1 = (bf16[3,128,2048]{2,1,0:T(8,128)(2,1)S(1)}, f32[1,1]{1,0:T(1,128)}, f32[1,1]{1,0:T(1,128)}, f32[1,1]{1,0:T(1,128)}) custom-call(bf16[128,2048]{1,0:T(8,128)(2,1)} %fp_in.1, bf16[128,2048]{1,0:T(8,128)(2,1)} %up_in.1, f32[1,2048]{1,0:T(1,128)} %bitcast.14, bf16[2048,256]{1,0:T(8,128)(2,1)} %wq_in.1, bf16[2048,128]{1,0:T(8,128)(2,1)} %wkv_in.1, ...), custom_call_target="tpu_custom_call" | custom-call | tf_op jit(solution)/shard_map/adjoint/pallas_call | solution.py:626
  87.5 0.0 copy-done
  87.5 3.2 %bitcast_add_fusion = f32[128,2048]{1,0:T(8,128)} fusion(bf16[128,2048]{1,0:T(8,128)(2,1)S(1)} %copy-done, bf16[3,128,2048]{2,1,0:T(8,128)(2,1)S(1)} %get-tuple-element.10, f32[]{:T(128)} %bitcast.5, f32[]{:T(128)} %bitcast.3, f32[]{:T(128)} %bitcast.1), kind=kLoop, calls=%fused_computation | loop fusion | flops 2621440 | bytes 3145740 | tf_op jit(solution)/shard_map/add | solution.py:651
Async XLA Ops:
  0.0 87.5 %copy-start = (bf16[128,2048]{1,0:T(8,128)(2,1)S(1)}, bf16[128,2048]{1,0:T(8,128)(2,1)}, u32[]{:S(2)}) copy-start(bf16[128,2048]{1,0:T(8,128)(2,1)} %up_in.1) | copy-start | bytes 1572868

commit v4 on v3

--- a/solution.py
+++ b/solution.py
@@ -60,6 +60,8 @@
     normed,
     inv,
     krylov,
+    gsend,
+    gbuf,
     pq_own,
     rs_send,
     rs_recv,
@@ -81,6 +83,8 @@
     rs_rsem,
     ag_ssem,
     ag_rsem,
+    g_ssem,
+    g_rsem,
     red_ssem,
     red_rsem,
 ):
@@ -100,6 +104,7 @@
     zl = lax.div(h, 2)
     c = lax.rem(h, 2)
     sibling = zl * 2 + (1 - c)
+    far = (1 - zl) * 2 + (1 - c)
     across = (1 - zl) * 2 + c
     mine = pl.ds(pl.multiple_of(h * part, part), part)
 
@@ -122,7 +127,7 @@
         pltpu.make_async_copy(wkv_in, wkv_of(h), in_sem.at[1]),
         pltpu.make_async_copy(wq_in, wq.at[c], in_sem.at[2]),
         pltpu.make_async_copy(up_in, xs.at[0], in_sem.at[3]),
-        pltpu.make_async_copy(wo_in, wo, in_sem.at[4]),
+        pltpu.make_async_copy(wo_in, wo.at[h], in_sem.at[4]),
     ]
     for load in loads:
         load.start()
@@ -228,6 +233,20 @@
     krylov[1:ITERS] = jnp.zeros((ITERS - 1,) + base_own.shape, F32)
     loads[4].wait()
 
+    def wo_copy(slot, owner, device):
+        return pltpu.make_async_remote_copy(
+            src_ref=wo.at[owner],
+            dst_ref=wo.at[owner],
+            send_sem=wkv_ssem.at[4 + slot],
+            recv_sem=wkv_rsem.at[4 + slot],
+            device_id=device,
+            device_id_type=MESH,
+        )
+
+    beside = (y * nz + lax.rem(zh + nz + 2 * zl - 1, nz)) * nx + x
+    wo_copy(0, h, (s, sibling)).start()
+    wo_copy(1, h, (beside, across)).start()
+
     def kt_copy(k, o, q):
         return pltpu.make_async_remote_copy(
             src_ref=kt_send.at[k, WIN - o, pl.ds(q * part, part), :],
@@ -280,11 +299,33 @@
             device_id_type=MESH,
         )
 
-    def gathered(k):
+    def ag_forward(k):
         ag_copy(k, 1, across, across).wait_recv()
         ag_copy(k, 2, across, sibling).start()
+
+    def ag_finish(k):
         ag_copy(k, 0, sibling, sibling).wait_recv()
         ag_copy(k, 2, sibling, sibling).wait_recv()
+
+    def g_copy(k, target):
+        return pltpu.make_async_remote_copy(
+            src_ref=gsend.at[k, target],
+            dst_ref=gbuf.at[k, mine, :],
+            send_sem=g_ssem.at[k],
+            recv_sem=g_rsem.at[k],
+            device_id=(s, target),
+            device_id_type=MESH,
+        )
+
+    def g_all(k):
+        return pltpu.make_async_remote_copy(
+            src_ref=gsend.at[k, pl.ds(0, GROUP - 1)],
+            dst_ref=gsend.at[k, pl.ds(0, GROUP - 1)],
+            send_sem=g_ssem.at[k],
+            recv_sem=g_rsem.at[k],
+            device_id=(s, sibling),
+            device_id_type=MESH,
+        )
 
     stages = (
         (red_a_send, red_a, nz * GROUP, zh * GROUP + h, z_peer),
@@ -385,16 +426,15 @@
         sp[j * rows : (j + 1) * rows, span:] = weights.astype(BF)
         ktr[:, j * rows : (j + 1) * rows] = block.astype(F32).T[0:edge, :].astype(BF)
 
-    def head_cotangents(k):
-        grad_out = dot(wo[...], xs[k], NT)
+    def spread_cotangents(grad_out, by_rows):
         terms = []
         for i in range(heads):
-            piece = grad_out[i * edge : (i + 1) * edge, :]
-            terms.append(
-                jnp.sum(piece * ao_t[i * edge : (i + 1) * edge, :], axis=0, keepdims=True)
-            )
+            entry = slice(i * edge, (i + 1) * edge)
+            piece = grad_out[entry, :]
+            terms.append(jnp.sum(piece * ao_t[entry, :], axis=0, keepdims=True))
             dopad[edge : 2 * edge, i * rows : (i + 1) * rows] = piece.astype(BF)
-            qd[span + i * rows : span + (i + 1) * rows, edge:] = piece.T.astype(BF)
+            turned = piece.T if by_rows is None else by_rows[:, entry]
+            qd[span + i * rows : span + (i + 1) * rows, edge:] = turned.astype(BF)
         return jnp.concatenate(terms, axis=1)
 
     def block_terms(k, low, high, row_terms):
@@ -460,6 +500,10 @@
             rs_copy(k, n).start()
             pq_own[:, half] = total[part:]
 
+        if not first:
+            ag_copy(k, 1, h, across).start()
+            ag_copy(k, 0, h, sibling).start()
+
         for o in range(1, WIN + 1):
 
             @pl.when(s + o < blocks)
@@ -478,6 +522,8 @@
         if first:
             wkv_copy(0, sibling, sibling).wait_recv()
             wkv_copy(2, sibling, sibling).wait_recv()
+            wo_copy(1, across, (s, across)).wait_recv()
+            wo_copy(2, across, (s, sibling)).start()
 
         hidden_grad = pq_own[...]
         for i in range(2):
@@ -493,12 +539,28 @@
         mapped = inv[:, 0:1] * (
             scaled - own_normed * jnp.mean(scaled * own_normed, axis=1, keepdims=True)
         )
-        xs[k + 1, mine, :] = mapped.astype(BF)
-        ag_copy(k + 1, 1, h, across).start()
-        ag_copy(k + 1, 0, h, sibling).start()
+        vector = mapped.astype(BF)
+
+        def share():
+            gsend[k, across] = dot(vector, wo[across], NT)
+            g_copy(k, across).start()
+            if first:
+                wo_copy(2, far, (s, sibling)).wait_recv()
+                wo_copy(0, sibling, (s, sibling)).wait_recv()
+            gsend[k, far] = dot(vector, wo[far], NT)
+            g_copy(k, far).start()
+            gsend[k, sibling] = dot(vector, wo[sibling], NT)
+            g_copy(k, sibling).start()
+            gbuf[k, mine, :] = dot(vector, wo[h], NT)
+
+        if first:
+            share()
+        else:
+            pl.when(k < ITERS - 1)(share)
+        xs[k + 1, mine, :] = vector
         krylov[k + 1] = mapped
 
-    row_terms = head_cotangents(0)
+    row_terms = spread_cotangents(dot(wo[h], xs[0], NT), None)
     for j in range(WIN, -1, -1):
         if j < WIN:
 
@@ -512,26 +574,39 @@
     finish(0, True)
 
     def step(k, carry):
-        gathered(k)
-        block_terms(k, 0, WIN + 1, head_cotangents(k))
+        g_all(k - 1).wait_recv()
+        by_rows = gbuf[k - 1]
+        block_terms(k, 0, WIN + 1, spread_cotangents(by_rows.T, by_rows))
         finish(k, False)
         return carry
 
     lax.fori_loop(1, ITERS, step, 0)
 
+    ag_copy(ITERS, 1, h, across).start()
+    ag_copy(ITERS, 0, h, sibling).start()
     add_inner(jnp.int32(ITERS), ITERS + 1)
     red_start(0, packed(gram[...]))
+    for k in range(1, ITERS):
+        ag_forward(k)
+    for k in range(1, ITERS):
+        ag_finish(k)
+    older = pltpu.make_async_copy(
+        xs.at[pl.ds(0, ITERS)], xs_out.at[pl.ds(0, ITERS)], in_sem.at[5]
+    )
+    older.start()
     total = red_finish(0)
     red_start(1, total)
-    gathered(ITERS)
-    kept = pltpu.make_async_copy(xs.at[pl.ds(1, ITERS)], xs_out, in_sem.at[5])
-    kept.start()
+    ag_forward(ITERS)
+    ag_finish(ITERS)
+    newest = pltpu.make_async_copy(xs.at[ITERS], xs_out.at[ITERS], in_sem.at[6])
+    newest.start()
     total = red_finish(1)
     red_start(2, total)
     factors = coefficients(red_finish(2))
     for i in range(ITERS):
         factor_outs[i][...] = factors[i + 1]
-    kept.wait()
+    older.wait()
+    newest.wait()
 
     for o in range(1, WIN + 1):
 
@@ -543,6 +618,11 @@
     wkv_copy(1, h, across).wait_send()
     wkv_copy(2, across, sibling).wait_send()
     wq_copy().wait_send()
+    wo_copy(0, h, (s, sibling)).wait_send()
+    wo_copy(1, h, (beside, across)).wait_send()
+    wo_copy(2, across, (s, sibling)).wait_send()
+    for k in range(ITERS - 1):
+        g_all(k).wait_send()
 
     for stage in range(3):
         red_all(stage).wait_send()
@@ -564,6 +644,22 @@
         return carry
 
     lax.fori_loop(0, ITERS, drain, 0)
+
+
+def combine(xs, factor_1, factor_2, factor_3, out, total, sem):
+    factors = (factor_1[...], factor_2[...], factor_3[...])
+    part = total.shape[0] // GROUP
+    copies = []
+    for q in range(GROUP):
+        here = pl.ds(q * part, part)
+        value = xs[0, here, :].astype(F32)
+        for i, factor in enumerate(factors):
+            value = value + factor * xs[i + 1, here, :].astype(F32)
+        total[here, :] = value
+        copies.append(pltpu.make_async_copy(total.at[here, :], out.at[here, :], sem.at[q]))
+        copies[-1].start()
+    for copy in copies:
+        copy.wait()
 
 
 def shards(dims, fixed_point, upstream, norm_gain, query_weight, keyval_weight, output_weight, log_norm, attention_out):
@@ -582,7 +678,7 @@
     scratch = [
         pltpu.VMEM((rows, width), BF),
         pltpu.VMEM((2, width, cols), BF),
-        pltpu.VMEM((cols, width), BF),
+        pltpu.VMEM((GROUP, cols, width), BF),
         pltpu.VMEM((2, width, 2 * kv_cols), BF),
         pltpu.VMEM((ITERS + 1, rows, width), BF),
         pltpu.VMEM((WIN + 1, rows, kv_cols), BF),
@@ -599,6 +695,8 @@
         state,
         pltpu.VMEM((part, 128), F32),
         pltpu.VMEM((ITERS + 1, part, width), F32),
+        pltpu.VMEM((ITERS - 1, GROUP, part, cols), F32),
+        pltpu.VMEM((ITERS - 1, rows, cols), F32),
         state,
         pltpu.VMEM((ITERS, 2, part, width // 2), BF),
         pltpu.VMEM((ITERS, 2, part, width // 2), BF),
@@ -612,21 +710,23 @@
         dma((7,)),
         dma((WIN,)),
         dma((WIN,)),
-        dma((4,)),
-        dma((4,)),
+        dma((7,)),
+        dma((7,)),
         dma((ITERS, WIN + 1)),
         dma((ITERS, WIN + 1)),
         dma((ITERS, 3)),
         dma((ITERS, 3)),
         dma((ITERS, 3)),
         dma((ITERS, 3)),
+        dma((ITERS - 1,)),
+        dma((ITERS - 1,)),
         dma((3,)),
         dma((3,)),
     ]
     images, *factors = pl.pallas_call(
         functools.partial(kernel, dims, float(entries)),
         out_shape=(
-            pltpu.VMEM((ITERS, rows, width), BF),
+            pltpu.VMEM((ITERS + 1, rows, width), BF),
         )
         + (jax.ShapeDtypeStruct((1, 1), F32),) * ITERS,
         in_specs=[hbm, hbm, vmem, hbm, hbm, hbm, vmem, vmem],
@@ -646,10 +746,15 @@
         log_norm,
         attention_out,
     )
-    total = upstream.astype(F32)
-    for i in range(ITERS):
-        total = total + factors[i] * images[i].astype(F32)
-    return total
+    return pl.pallas_call(
+        combine,
+        out_shape=jax.ShapeDtypeStruct((rows, width), F32),
+        in_specs=[vmem] * (ITERS + 1),
+        out_specs=hbm,
+        scratch_shapes=[pltpu.VMEM((rows, width), F32), dma((GROUP,))],
+        compiler_params=pltpu.CompilerParams(vmem_limit_bytes=8 << 20),
+        name="combine",
+    )(images, *factors)
 
 
 def solution(mesh, dims=(4, 4, 8)):

time: 91.4 us -> 98.3 us (1.075)
  Pallas kernels: 87.5 us -> 97.8 us
  other arithmetic: 3.2 us -> 0 us
    pallas_call x1, Pallas kernels: 87.5 us -> 94.7 us  [shards(): pl.pallas_call(functools.partial(kernel, dims, float(entries)), out_shape...]
    add x1 -> x0, other arithmetic: 3.2 us -> none  [shards(): total = total + factors[i] * images[i].astype(F32)]
    pallas_call x0 -> x1, Pallas kernels: none -> 3.08 us  [shards(): pl.pallas_call(combine, out_shape=jax.ShapeDtypeStruct((rows, width), F32...]
where the time goes in v4:
time: 98.3 us; the launch traced here: 97.8 us
  Pallas kernels  97.8 us (99%)
    pallas_call x1, Pallas kernels, shards(): pl.pallas_call(functools.partial(kernel, dims, float(entries)), out_shape...  94.7 us
    pallas_call x1, Pallas kernels, shards(): pl.pallas_call(combine, out_shape=jax.ShapeDtypeStruct((rows, width), F32...  3.08 us

profile of v4, /device:TPU:1, one launch (start us, length us, event | category | flops | bytes accessed | tf_op | source)
XLA Modules:
  0.0 97.8 jit_solution(7957854770589269548)
XLA Ops:
  0.0 94.7 %adjoint.1 = (bf16[4,128,2048]{2,1,0:T(8,128)(2,1)S(1)}, f32[1,1]{1,0:T(1,128)}, f32[1,1]{1,0:T(1,128)}, f32[1,1]{1,0:T(1,128)}) custom-call(bf16[128,2048]{1,0:T(8,128)(2,1)} %fp_in.1, bf16[128,2048]{1,0:T(8,128)(2,1)} %up_in.1, f32[1,2048]{1,0:T(1,128)} %bitcast.1, bf16[2048,256]{1,0:T(8,128)(2,1)} %wq_in.1, bf16[2048,128]{1,0:T(8,128)(2,1)} %wkv_in.1, ...), custom_call_target="tpu_custom_call" | custom-call | tf_op jit(solution)/shard_map/adjoint/pallas_call | solution.py:726
  94.7 3.1 %combine.1 = f32[128,2048]{1,0:T(8,128)} custom-call(bf16[4,128,2048]{2,1,0:T(8,128)(2,1)S(1)} %get-tuple-element.9.xs, f32[1,1]{1,0:T(1,128)} %get-tuple-element.10.factor_1, f32[1,1]{1,0:T(1,128)} %get-tuple-element.11.factor_2, f32[1,1]{1,0:T(1,128)} %get-tuple-element.12.factor_3), custom_call_target="tpu_custom_call" | custom-call | tf_op jit(solution)/shard_map/combine/pallas_call | solution.py:749

commit v5 on v3

--- a/solution.py
+++ b/solution.py
@@ -38,9 +38,7 @@
     ln_ref,
     ao_ref,
     xs_out,
-    factor_1,
-    factor_2,
-    factor_3,
+    factors_out,
     fp,
     wq,
     wo,
@@ -84,7 +82,6 @@
     red_ssem,
     red_rsem,
 ):
-    factor_outs = (factor_1, factor_2, factor_3)
     nx, nz, ny = dims
     blocks = nx * nz * ny
     rows, width = fp.shape
@@ -100,6 +97,7 @@
     zl = lax.div(h, 2)
     c = lax.rem(h, 2)
     sibling = zl * 2 + (1 - c)
+    far = (1 - zl) * 2 + (1 - c)
     across = (1 - zl) * 2 + c
     mine = pl.ds(pl.multiple_of(h * part, part), part)
 
@@ -181,11 +179,25 @@
             device_id_type=MESH,
         )
 
-    for o in range(WIN, 0, -1):
-
-        @pl.when(s + o < blocks)
+    @pl.when(s + WIN < blocks)
+    def _():
+        kv_copy(WIN).start()
+
+    for o in range(1, WIN):
+
+        @pl.when(x + o < nx)
         def _(o=o):
             kv_copy(o).start()
+
+    def kv_relay(d):
+        return pltpu.make_async_remote_copy(
+            src_ref=kvwin.at[0],
+            dst_ref=kvwin.at[d],
+            send_sem=kv_ssem.at[WIN + d - 1],
+            recv_sem=kv_rsem.at[WIN - d - 1],
+            device_id=(s - d, h),
+            device_id_type=MESH,
+        )
 
     def wkv_copy(slot, owner, target):
         return pltpu.make_async_remote_copy(
@@ -270,21 +282,27 @@
         )
 
     def ag_copy(k, slot, owner, target):
-        span = pl.ds(pl.multiple_of(owner * part, part), part)
-        return pltpu.make_async_remote_copy(
-            src_ref=xs.at[k, span, :],
-            dst_ref=xs.at[k, span, :],
+        most = width * 3 // 4
+        columns = (pl.ds(0, width), pl.ds(0, most), pl.ds(0, most))[slot] if slot < 3 else pl.ds(most, width - most)
+        piece = xs.at[k, pl.ds(pl.multiple_of(owner * part, part), part), columns]
+        return pltpu.make_async_remote_copy(
+            src_ref=piece,
+            dst_ref=piece,
             send_sem=ag_ssem.at[k - 1, slot],
             recv_sem=ag_rsem.at[k - 1, slot],
             device_id=(s, target),
             device_id_type=MESH,
         )
+
+    own_slices = ((1, across), (3, far), (4, across), (0, sibling))
 
     def gathered(k):
         ag_copy(k, 1, across, across).wait_recv()
         ag_copy(k, 2, across, sibling).start()
         ag_copy(k, 0, sibling, sibling).wait_recv()
-        ag_copy(k, 2, sibling, sibling).wait_recv()
+        ag_copy(k, 4, across, across).wait_recv()
+        ag_copy(k, 3, far, far).wait_recv()
+        ag_copy(k, 2, far, sibling).wait_recv()
 
     stages = (
         (red_a_send, red_a, nz * GROUP, zh * GROUP + h, z_peer),
@@ -494,17 +512,23 @@
             scaled - own_normed * jnp.mean(scaled * own_normed, axis=1, keepdims=True)
         )
         xs[k + 1, mine, :] = mapped.astype(BF)
-        ag_copy(k + 1, 1, h, across).start()
-        ag_copy(k + 1, 0, h, sibling).start()
+        for slot, target in own_slices:
+            ag_copy(k + 1, slot, h, target).start()
         krylov[k + 1] = mapped
 
     row_terms = head_cotangents(0)
-    for j in range(WIN, -1, -1):
+    for j in (WIN, 0, *range(WIN - 1, 0, -1)):
         if j < WIN:
 
             @pl.when(s >= WIN - j)
             def _(j=j):
                 kv_copy(WIN - j).wait_recv()
+                if j == 0:
+                    for d in range(1, WIN):
+
+                        @pl.when(x >= d)
+                        def _(d=d):
+                            kv_relay(d).start()
 
         probabilities(j)
         block_terms(0, j, j + 1, row_terms)
@@ -519,25 +543,38 @@
 
     lax.fori_loop(1, ITERS, step, 0)
 
+    older = pltpu.make_async_copy(
+        xs.at[pl.ds(0, ITERS)], xs_out.at[pl.ds(0, ITERS)], in_sem.at[5]
+    )
+    older.start()
     add_inner(jnp.int32(ITERS), ITERS + 1)
     red_start(0, packed(gram[...]))
     total = red_finish(0)
     red_start(1, total)
     gathered(ITERS)
-    kept = pltpu.make_async_copy(xs.at[pl.ds(1, ITERS)], xs_out, in_sem.at[5])
-    kept.start()
+    newest = pltpu.make_async_copy(xs.at[ITERS], xs_out.at[ITERS], in_sem.at[6])
+    newest.start()
     total = red_finish(1)
     red_start(2, total)
     factors = coefficients(red_finish(2))
     for i in range(ITERS):
-        factor_outs[i][...] = factors[i + 1]
-    kept.wait()
-
-    for o in range(1, WIN + 1):
-
-        @pl.when(s + o < blocks)
+        factors_out[8 * i : 8 * (i + 1), :] = jnp.broadcast_to(factors[i + 1], (8, 128))
+    older.wait()
+    newest.wait()
+
+    @pl.when(s + WIN < blocks)
+    def _():
+        kv_copy(WIN).wait_send()
+
+    for o in range(1, WIN):
+
+        @pl.when(x + o < nx)
         def _(o=o):
             kv_copy(o).wait_send()
+
+        @pl.when((s >= WIN) & (x >= o))
+        def _(o=o):
+            kv_relay(o).wait_send()
 
     wkv_copy(0, h, sibling).wait_send()
     wkv_copy(1, h, across).wait_send()
@@ -558,12 +595,28 @@
         gq_copy(k).wait_send()
         rs_copy(k, 0).wait_send()
         rs_copy(k, 1).wait_send()
-        ag_copy(k + 1, 0, h, sibling).wait_send()
-        ag_copy(k + 1, 1, h, across).wait_send()
+        for slot, target in own_slices:
+            ag_copy(k + 1, slot, h, target).wait_send()
         ag_copy(k + 1, 2, across, sibling).wait_send()
         return carry
 
     lax.fori_loop(0, ITERS, drain, 0)
+
+
+def combine(xs, factors_in, out, total, sem):
+    factors = [factors_in[8 * i : 8 * i + 1, 0:1] for i in range(ITERS)]
+    part = total.shape[0] // GROUP
+    copies = []
+    for q in range(GROUP):
+        here = pl.ds(q * part, part)
+        value = xs[0, here, :].astype(F32)
+        for i, factor in enumerate(factors):
+            value = value + factor * xs[i + 1, here, :].astype(F32)
+        total[here, :] = value
+        copies.append(pltpu.make_async_copy(total.at[here, :], out.at[here, :], sem.at[q]))
+        copies[-1].start()
+    for copy in copies:
+        copy.wait()
 
 
 def shards(dims, fixed_point, upstream, norm_gain, query_weight, keyval_weight, output_weight, log_norm, attention_out):
@@ -610,7 +663,7 @@
         pltpu.VMEM((ny, 1, 128), F32),
         pltpu.VMEM((16, 128), F32),
         dma((7,)),
-        dma((WIN,)),
+        dma((2 * WIN - 1,)),
         dma((WIN,)),
         dma((4,)),
         dma((4,)),
@@ -618,19 +671,19 @@
         dma((ITERS, WIN + 1)),
         dma((ITERS, 3)),
         dma((ITERS, 3)),
-        dma((ITERS, 3)),
-        dma((ITERS, 3)),
+        dma((ITERS, 5)),
+        dma((ITERS, 5)),
         dma((3,)),
         dma((3,)),
     ]
-    images, *factors = pl.pallas_call(
+    images, factors = pl.pallas_call(
         functools.partial(kernel, dims, float(entries)),
         out_shape=(
-            pltpu.VMEM((ITERS, rows, width), BF),
-        )
-        + (jax.ShapeDtypeStruct((1, 1), F32),) * ITERS,
+            pltpu.VMEM((ITERS + 1, rows, width), BF),
+        )
+        + (pltpu.VMEM((8 * ITERS, 128), F32),),
         in_specs=[hbm, hbm, vmem, hbm, hbm, hbm, vmem, vmem],
-        out_specs=(vmem,) + (vmem,) * ITERS,
+        out_specs=(vmem, vmem),
         scratch_shapes=scratch,
         compiler_params=pltpu.CompilerParams(
             collective_id=0, has_side_effects=True, vmem_limit_bytes=58 << 20
@@ -646,10 +699,15 @@
         log_norm,
         attention_out,
     )
-    total = upstream.astype(F32)
-    for i in range(ITERS):
-        total = total + factors[i] * images[i].astype(F32)
-    return total
+    return pl.pallas_call(
+        combine,
+        out_shape=jax.ShapeDtypeStruct((rows, width), F32),
+        in_specs=[vmem, vmem],
+        out_specs=hbm,
+        scratch_shapes=[pltpu.VMEM((rows, width), F32), dma((GROUP,))],
+        compiler_params=pltpu.CompilerParams(vmem_limit_bytes=8 << 20),
+        name="combine",
+    )(images, factors)
 
 
 def solution(mesh, dims=(4, 4, 8)):

time: 91.4 us -> 89.2 us (0.976)
  other arithmetic: 3.2 us -> 0 us
  Pallas kernels: 87.5 us -> 88.8 us
    add x1 -> x0, other arithmetic: 3.2 us -> none  [shards(): total = total + factors[i] * images[i].astype(F32)]
    pallas_call x0 -> x1, Pallas kernels: none -> 1.24 us  [shards(): pl.pallas_call(combine, out_shape=jax.ShapeDtypeStruct((rows, width), F32...]
where the time goes in v5:
time: 89.2 us; the launch traced here: 88.8 us
  Pallas kernels  88.8 us (100%)
    pallas_call x1, Pallas kernels, shards(): pl.pallas_call(functools.partial(kernel, dims, float(entries)), out_shape...  87.5 us

profile of v5, /device:TPU:1, one launch (start us, length us, event | category | flops | bytes accessed | tf_op | source)
XLA Modules:
  0.0 88.8 jit_solution(4234562622070124904)
XLA Ops:
  0.0 87.5 %adjoint.1 = (bf16[4,128,2048]{2,1,0:T(8,128)(2,1)S(1)}, f32[24,128]{1,0:T(8,128)S(1)}) custom-call(bf16[128,2048]{1,0:T(8,128)(2,1)} %fp_in.1, bf16[128,2048]{1,0:T(8,128)(2,1)} %up_in.1, f32[1,2048]{1,0:T(1,128)} %bitcast.1, bf16[2048,256]{1,0:T(8,128)(2,1)} %wq_in.1, bf16[2048,128]{1,0:T(8,128)(2,1)} %wkv_in.1, bf16[256,2048]{1,0:T(8,128)(2,1)} %wo_in.1, ...), custom_call_target="tpu_custom_call" | custom-call | tf_op jit(solution)/shard_map/adjoint/pallas_call | solution.py:679
  87.6 1.2 %combine.1 = f32[128,2048]{1,0:T(8,128)} custom-call(bf16[4,128,2048]{2,1,0:T(8,128)(2,1)S(1)} %get-tuple-element.7.xs, f32[24,128]{1,0:T(8,128)S(1)} %get-tuple-element.8.factors_in), custom_call_target="tpu_custom_call" | custom-call | tf_op jit(solution)/shard_map/combine/pallas_call | solution.py:702

commit v6 on v5

--- a/solution.py
+++ b/solution.py
@@ -199,18 +199,18 @@
             device_id_type=MESH,
         )
 
-    def wkv_copy(slot, owner, target):
+    beside = (y * nz + lax.rem(zh + nz + 2 * zl - 1, nz)) * nx + x
+
+    def wkv_copy(slot, owner, target, block):
         return pltpu.make_async_remote_copy(
             src_ref=wkv_of(owner),
             dst_ref=wkv_of(owner),
             send_sem=wkv_ssem.at[slot],
             recv_sem=wkv_rsem.at[slot],
-            device_id=(s, target),
-            device_id_type=MESH,
-        )
-
-    wkv_copy(0, h, sibling).start()
-    wkv_copy(1, h, across).start()
+            device_id=(block, target),
+            device_id_type=MESH,
+        )
+
 
     loads[2].wait()
 
@@ -305,9 +305,9 @@
         ag_copy(k, 2, far, sibling).wait_recv()
 
     stages = (
+        (red_c_send, red_c, ny, y, y_peer),
+        (red_b_send, red_b, nx, x, x_peer),
         (red_a_send, red_a, nz * GROUP, zh * GROUP + h, z_peer),
-        (red_b_send, red_b, nx, x, x_peer),
-        (red_c_send, red_c, ny, y, y_peer),
     )
 
     def red_all(stage):
@@ -463,8 +463,6 @@
         gq_copy(k).start()
         add_inner(jnp.int32(k), ITERS)
         if first:
-            wkv_copy(1, across, across).wait_recv()
-            wkv_copy(2, across, sibling).start()
             wq_copy().wait_recv()
         gq_copy(k).wait_recv()
         theirs = pl.ds(pl.multiple_of(across * part, part), part)
@@ -478,6 +476,10 @@
             rs_copy(k, n).start()
             pq_own[:, half] = total[part:]
 
+        if first:
+            wkv_copy(1, across, across, s).wait_recv()
+            wkv_copy(2, across, sibling, s).start()
+
         for o in range(1, WIN + 1):
 
             @pl.when(s + o < blocks)
@@ -494,8 +496,8 @@
             collected.append(total.astype(BF))
 
         if first:
-            wkv_copy(0, sibling, sibling).wait_recv()
-            wkv_copy(2, sibling, sibling).wait_recv()
+            wkv_copy(0, sibling, sibling, s).wait_recv()
+            wkv_copy(2, sibling, sibling, s).wait_recv()
 
         hidden_grad = pq_own[...]
         for i in range(2):
@@ -530,6 +532,9 @@
                         def _(d=d):
                             kv_relay(d).start()
 
+        if j == 0:
+            wkv_copy(0, h, sibling, s).start()
+            wkv_copy(1, h, across, beside).start()
         probabilities(j)
         block_terms(0, j, j + 1, row_terms)
     gram[...] = jnp.zeros_like(gram)
@@ -537,7 +542,9 @@
 
     def step(k, carry):
         gathered(k)
-        block_terms(k, 0, WIN + 1, head_cotangents(k))
+        row_terms = head_cotangents(k)
+        block_terms(k, 0, 2, row_terms)
+        block_terms(k, 2, WIN + 1, row_terms)
         finish(k, False)
         return carry
 
@@ -576,9 +583,9 @@
         def _(o=o):
             kv_relay(o).wait_send()
 
-    wkv_copy(0, h, sibling).wait_send()
-    wkv_copy(1, h, across).wait_send()
-    wkv_copy(2, across, sibling).wait_send()
+    wkv_copy(0, h, sibling, s).wait_send()
+    wkv_copy(1, h, across, beside).wait_send()
+    wkv_copy(2, across, sibling, s).wait_send()
     wq_copy().wait_send()
 
     for stage in range(3):

time: 89.2 us -> 87.9 us (0.985)
  Pallas kernels: 88.8 us -> 87.7 us
    pallas_call x1, Pallas kernels: 87.5 us -> 86.5 us  [shards(): pl.pallas_call(functools.partial(kernel, dims, float(entries)), out_shape...]
where the time goes in v6:
time: 87.9 us; the launch traced here: 87.7 us
  Pallas kernels  87.7 us (100%)
    pallas_call x1, Pallas kernels, shards(): pl.pallas_call(functools.partial(kernel, dims, float(entries)), out_shape...  86.5 us

profile of v6, /device:TPU:1, one launch (start us, length us, event | category | flops | bytes accessed | tf_op | source)
XLA Modules:
  0.0 87.7 jit_solution(15778179082003313304)
XLA Ops:
  0.0 86.5 %adjoint.1 = (bf16[4,128,2048]{2,1,0:T(8,128)(2,1)S(1)}, f32[24,128]{1,0:T(8,128)S(1)}) custom-call(bf16[128,2048]{1,0:T(8,128)(2,1)} %fp_in.1, bf16[128,2048]{1,0:T(8,128)(2,1)} %up_in.1, f32[1,2048]{1,0:T(1,128)} %bitcast.1, bf16[2048,256]{1,0:T(8,128)(2,1)} %wq_in.1, bf16[2048,128]{1,0:T(8,128)(2,1)} %wkv_in.1, bf16[256,2048]{1,0:T(8,128)(2,1)} %wo_in.1, ...), custom_call_target="tpu_custom_call" | custom-call | tf_op jit(solution)/shard_map/adjoint/pallas_call | solution.py:686
  86.5 1.2 %combine.1 = f32[128,2048]{1,0:T(8,128)} custom-call(bf16[4,128,2048]{2,1,0:T(8,128)(2,1)S(1)} %get-tuple-element.7.xs, f32[24,128]{1,0:T(8,128)S(1)} %get-tuple-element.8.factors_in), custom_call_target="tpu_custom_call" | custom-call | tf_op jit(solution)/shard_map/combine/pallas_call | solution.py:709
